TPU v7x, 128 devices: a whole 4x4x4 slice. The times are simulated.
128 devices in a mesh: cluster: 4 (over z), sub: 32 (over y, x, core).
Axes of the slice: x: 4, y: 4, z: 4, core: 2. Of those that a mesh axis runs over, the one named last changes fastest.
Arguments:
- dual_operators: bfloat16 [256, 2048, 2048], P(('cluster', 'sub')), may hold values from -1 to 3, as said below
- local_loads: float32 [256, 2048, 128], P(('cluster', 'sub')), may hold values from -15 to 15
- modes: float32 [256, 6, 2048], P(('cluster', 'sub')), may hold values from -4 to 4
- coarse_matrix: float32 [1536, 1536], P(('cluster', 'sub')), may hold values from -1 to 1, as said below
- coarse_loads: float32 [1536, 128], replicated, may hold values from -6144 to 6144
- slot_block: int32 [128, 32], P(('cluster', 'sub')), may hold values from 0 to 31, each once within a row
Outputs:
- multipliers: float32 [256, 2048, 128], P(('cluster', 'sub'))
- projected_residual: float32 [256, 2048, 128], P(('cluster', 'sub'))
Inputs may be any that keep to these rules, and one draw needn't show every extreme that they name: `dual_operators`: each subdomain's matrix is symmetric and positive definite. `coarse_matrix`: Symmetric.
All inputs are finite; a program needn't handle non-finite values.
Results may differ from a plain program's by a relative error of at most 0.0018.
Values sent between devices are 32-bit elements; how exact they have to be, the bound alone decides.
No kernel may reach another device: no remote copies, remote signals or barrier semaphores. Data moves between devices by JAX's collectives and lax.ppermute only.
A program may use at most 128 MiB of HBM per device.

v0:
```python
import jax
import jax.numpy as jnp
from jax import lax
from jax.sharding import PartitionSpec as P

NMODE = 6
ITERS = 3


def from_behind(value, axis, steps):
    count = lax.axis_size(axis)
    initial, last = (max(0, -steps), min(count, count - steps))
    return lax.ppermute(value, axis, [(source, source + steps) for source in range(initial, last)])


def on_device(dual_operators, local_loads, modes, coarse_matrix, coarse_loads, slot_block):
    highest = lax.Precision.HIGHEST
    slot_order = slot_block[0]
    block_total = slot_order.shape[0]
    face_size = block_total // 8
    local_count, dual_order, load_count = local_loads.shape
    block_count = block_total // local_count
    block_size = dual_order // block_count
    peer_count = lax.axis_size("sub")
    cluster_total = lax.axis_size("cluster")
    own_index = lax.axis_index("sub")
    cluster_index = lax.axis_index("cluster")
    positions = jnp.arange(block_total, dtype=jnp.int32)
    inverse = jnp.sum(
        positions[:, None] * (slot_order[:, None] == positions[None, :]).astype(jnp.int32), axis=0
    )
    face_ids = positions // face_size
    shared = (
        (face_ids == 0) & (own_index > 0)
        | (face_ids == 1) & (own_index < peer_count - 1)
        | (face_ids == 2) & (cluster_index > 0)
        | (face_ids == 3) & (cluster_index < cluster_total - 1)
        | (face_ids >= 6)
    )
    slot_weights = jnp.where(shared, 0.5, 1.0).astype(jnp.float32)
    weights = jnp.repeat(slot_weights[inverse], block_size).reshape(local_count, dual_order)
    coeff_rows = local_count * NMODE

    def to_slots(values):
        return values.reshape(block_total, block_size, values.shape[-1])[slot_order]

    def from_slots(slot_values):
        return slot_values[inverse].reshape(local_count, dual_order, slot_values.shape[-1])

    def receive(slot_values):
        trailing = slot_values.shape[1:]
        outer = slot_values[: 4 * face_size].reshape((4, face_size) + trailing)
        lower_sub = from_behind(outer[1], "sub", 1)
        upper_sub = from_behind(outer[0], "sub", -1)
        lower_cluster = from_behind(outer[3], "cluster", 1)
        upper_cluster = from_behind(outer[2], "cluster", -1)
        blank_faces = jnp.zeros((2 * face_size,) + trailing, jnp.float32)
        return jnp.concatenate(
            [
                lower_sub,
                upper_sub,
                lower_cluster,
                upper_cluster,
                blank_faces,
                slot_values[7 * face_size : 8 * face_size],
                slot_values[6 * face_size : 7 * face_size],
            ],
            axis=0,
        )

    def assemble(values):
        sent = to_slots(values)
        return from_slots(sent - receive(sent))

    def apply_dual(direction):
        local_image = jnp.einsum(
            "smn,snl->sml",
            dual_operators,
            direction.astype(jnp.bfloat16),
            preferred_element_type=jnp.float32,
        )
        return assemble(local_image)

    def spread_modes(coeff):
        return jnp.einsum(
            "srm,srl->sml", modes, coeff.reshape(local_count, NMODE, load_count), precision=highest
        )

    def coarse_coefficients(values):
        coarse_terms = jnp.einsum("srm,sml->srl", modes, values, precision=highest).reshape(
            coeff_rows, load_count
        )
        return jnp.dot(
            coarse_matrix,
            lax.all_gather(coarse_terms, ("cluster", "sub"), axis=0, tiled=True),
            precision=highest,
        )

    def inner_product(left, right):
        return jnp.sum(weights[:, :, None] * left * right, axis=(0, 1))

    def residual_norm(values):
        return lax.psum(inner_product(values, values), ("cluster", "sub"))

    def correct(coeff):
        return assemble(spread_modes(coeff))

    initial_coeff = jnp.dot(coarse_matrix, coarse_loads, precision=highest)
    combined = assemble(jnp.concatenate([local_loads, spread_modes(initial_coeff)], axis=2))
    dual_rhs = combined[:, :, :load_count]
    multipliers = combined[:, :, load_count:]
    residual = dual_rhs - apply_dual(multipliers)
    projected = residual - correct(coarse_coefficients(residual))
    gamma_now = residual_norm(projected)
    direction = projected
    for iteration in range(ITERS):
        image_dir = apply_dual(direction)
        curvature_sum = lax.psum(inner_product(direction, image_dir), ("cluster", "sub"))
        step_size = gamma_now / curvature_sum
        multipliers = multipliers + step_size * direction
        residual = residual - step_size * image_dir
        projected = residual - correct(coarse_coefficients(residual))
        if iteration + 1 < ITERS:
            gamma_next = residual_norm(projected)
            direction = projected + gamma_next / gamma_now * direction
            gamma_now = gamma_next
    return (multipliers, projected)


def solution(mesh):
    return jax.shard_map(
        on_device,
        mesh=mesh,
        in_specs=(
            P(("cluster", "sub"), None, None),
            P(("cluster", "sub"), None, None),
            P(("cluster", "sub"), None, None),
            P(("cluster", "sub"), None),
            P(),
            P(("cluster", "sub"), None),
        ),
        out_specs=(P(("cluster", "sub"), None, None), P(("cluster", "sub"), None, None)),
        check_vma=False,
    )
```

profile of v0, /device:TPU:1, one launch (start us, length us, event | category | flops | bytes accessed | tf_op | source)
XLA Modules:
  0.0 927.4 jit_solution(14843520013973359392)
XLA Ops:
  9.8 5.3 copy.102
  15.2 5.0 gather_fusion
  21.8 4.5 collective-permute-start
  28.3 3.6 collective-permute-start.2
  33.2 3.9 collective-permute-done.1
  37.2 5.0 collective-permute-done.2
  42.2 4.1 collective-permute-done.3
  49.2 5.0 gather_fusion.1
  54.3 4.5 fusion.20
  60.7 13.5 %convolution_bitcast_fusion.7 = f32[2,2048,128]{1,2,0:T(8,128)} fusion(bf16[2,2048,2048]{2,1,0:T(8,128)(2,1)} %param.6, f32[2,2048,128]{1,2,0:T(8,128)S(1)} %copy.142), kind=kOutput, calls=%fused_computation.31 | convolution fusion | flops 2148007936 | bytes 20971520 | tf_op jit(solution)/shard_map/smn,snl->sml/dot_general | solution.py:76
  80.4 5.0 collective-permute-start.4
  87.3 3.4 collective-permute-start.6
  95.4 3.1 collective-permute-done.7
  100.2 3.6 gather_fusion.4
  103.8 3.0 copy.106
  112.0 39.0 %all-gather = f32[128,12,128]{2,1,0:T(8,128)S(1)} all-gather(f32[1,12,128]{2,1,0:T(8,128)S(1)} %reshape.396), channel_id=1, replica_groups=mesh['cluster'=4,'sub'=32] {'cluster','sub'}, dimensions={0}, use_global_device_ids=true | all-gather | bytes 792576 | tf_op jit(solution)/shard_map/all_gather | solution.py:95
  171.5 3.8 collective-permute-done.11
  183.6 13.5 %convolution_bitcast_fusion.5 = f32[2,2048,128]{1,2,0:T(8,128)} fusion(bf16[2,2048,2048]{2,1,0:T(8,128)(2,1)} %param.6, f32[2,2048,128]{1,2,0:T(8,128)S(1)} %sub.70), kind=kOutput, calls=%fused_computation.29 | convolution fusion | flops 2148007936 | bytes 20971520 | tf_op jit(solution)/shard_map/smn,snl->sml/dot_general | solution.py:76
  200.0 3.6 gather_fusion.7
  205.7 3.3 collective-permute-start.12
  215.6 4.8 collective-permute-done.13
  220.5 3.6 collective-permute-done.15
  225.9 3.6 gather_fusion.8
  234.4 64.9 %all-reduce = (f32[128]{0:T(128)S(1)}, f32[128]{0:T(128)S(1)}) all-reduce(f32[128]{0:T(128)S(1)} %get-tuple-element.11, f32[128]{0:T(128)S(1)} %get-tuple-element.10), channel_id=1, replica_groups=mesh['cluster'=4,'sub'=32] {'cluster','sub'}, use_global_device_ids=true, to_apply=%region_2.3 | all-reduce | flops 256 | bytes 2048 | tf_op jit(solution)/shard_map/psum | solution.py:103
  303.9 37.9 %all-gather.1 = f32[128,12,128]{2,1,0:T(8,128)} all-gather(f32[1,12,128]{2,1,0:T(8,128)S(1)} %reshape.398), channel_id=1, replica_groups=mesh['cluster'=4,'sub'=32] {'cluster','sub'}, dimensions={0}, use_global_device_ids=true | all-gather | bytes 792576 | tf_op jit(solution)/shard_map/all_gather | solution.py:95
  345.7 3.2 convolution_bitcast_fusion.4
  351.8 3.6 gather_fusion.9
  361.5 3.2 collective-permute-start.18
  367.2 3.4 collective-permute-done.18
  370.7 4.1 collective-permute-done.19
  376.5 3.6 gather_fusion.10
  383.0 3.3 fusion.2
  386.3 62.8 %psum.44 = f32[128]{0:T(128)S(1)} all-reduce(f32[128]{0:T(128)S(1)} %get-tuple-element.16), channel_id=1, replica_groups=mesh['cluster'=4,'sub'=32] {'cluster','sub'}, use_global_device_ids=true, to_apply=%region_6.7 | all-reduce | flops 128 | bytes 1024 | tf_op jit(solution)/shard_map/psum | solution.py:103
  451.8 12.7 %convolution_bitcast_fusion.3 = f32[2,2048,128]{1,2,0:T(8,128)} fusion(bf16[2,2048,2048]{2,1,0:T(8,128)(2,1)} %param.6, f32[2,2048,128]{1,2,0:T(8,128)S(1)} %multiply_add_fusion.2), kind=kOutput, calls=%fused_computation.27 | convolution fusion | flops 2148007936 | bytes 20971520 | tf_op jit(solution)/shard_map/smn,snl->sml/dot_general | solution.py:76
  467.4 3.6 gather_fusion.11
  472.5 3.2 collective-permute-start.20
  486.3 4.1 collective-permute-done.23
  492.0 3.6 gather_fusion.12
  500.5 63.2 %psum.45 = f32[128]{0:T(128)S(1)} all-reduce(f32[128]{0:T(128)S(1)} %multiply_reduce_fusion.1), channel_id=1, replica_groups=mesh['cluster'=4,'sub'=32] {'cluster','sub'}, use_global_device_ids=true, to_apply=%region_8.9 | all-reduce | flops 128 | bytes 1024 | tf_op jit(solution)/shard_map/psum | solution.py:118
  569.6 38.3 %all-gather.2 = f32[128,12,128]{2,1,0:T(8,128)} all-gather(f32[1,12,128]{2,1,0:T(8,128)S(1)} %reshape.400), channel_id=1, replica_groups=mesh['cluster'=4,'sub'=32] {'cluster','sub'}, dimensions={0}, use_global_device_ids=true | all-gather | bytes 792576 | tf_op jit(solution)/shard_map/all_gather | solution.py:95
  611.7 3.2 convolution_bitcast_fusion.2
  617.9 3.6 gather_fusion.13
  633.4 3.1 collective-permute-done.26
  636.4 4.1 collective-permute-done.27
  642.2 3.6 gather_fusion.14
  648.7 4.1 fusion.3
  652.8 63.0 %psum.46 = f32[128]{0:T(128)S(1)} all-reduce(f32[128]{0:T(128)S(1)} %get-tuple-element.14), channel_id=1, replica_groups=mesh['cluster'=4,'sub'=32] {'cluster','sub'}, use_global_device_ids=true, to_apply=%region_10.11 | all-reduce | flops 128 | bytes 1024 | tf_op jit(solution)/shard_map/psum | solution.py:103
  715.8 13.5 %convolution_bitcast_fusion.1 = f32[2,2048,128]{1,2,0:T(8,128)} fusion(bf16[2,2048,2048]{2,1,0:T(8,128)(2,1)} %param.6, f32[2,2048,128]{1,2,0:T(8,128)} %get-tuple-element.15, f32[2,2048,128]{1,2,0:T(8,128)S(1)} %multiply_add_fusion.2, f32[128]{0:T(128)S(1)} %div.36), kind=kOutput, calls=%fused_computation.25 | convolution fusion | flops 2149056512 | bytes 23069184 | tf_op jit(solution)/shard_map/smn,snl->sml/dot_general | solution.py:76
  732.2 3.7 gather_fusion.15
  748.0 3.1 collective-permute-done.30
  751.1 4.1 collective-permute-done.31
  756.9 3.7 gather_fusion.16
  766.3 63.4 %psum.47 = f32[128]{0:T(128)S(1)} all-reduce(f32[128]{0:T(128)S(1)} %multiply_reduce_fusion), channel_id=1, replica_groups=mesh['cluster'=4,'sub'=32] {'cluster','sub'}, use_global_device_ids=true, to_apply=%region_12.13 | all-reduce | flops 128 | bytes 1024 | tf_op jit(solution)/shard_map/psum | solution.py:118
  829.7 4.3 convolution_bitcast_fusion.10
  834.0 38.0 %all-gather.3 = f32[128,12,128]{2,1,0:T(8,128)} all-gather(f32[1,12,128]{2,1,0:T(8,128)S(1)} %reshape.402), channel_id=1, replica_groups=mesh['cluster'=4,'sub'=32] {'cluster','sub'}, dimensions={0}, use_global_device_ids=true | all-gather | bytes 792576 | tf_op jit(solution)/shard_map/all_gather | solution.py:95
  875.9 3.2 convolution_bitcast_fusion
  879.1 3.0 copy.134
  882.1 3.6 gather_fusion.17
  891.6 3.5 collective-permute-start.34
  897.4 3.7 collective-permute-done.34
  901.1 4.1 collective-permute-done.35
  907.0 3.7 gather_fusion.18
  913.6 8.8 fusion.8
  922.3 3.0 copy.137
  (232 shorter events, 204.0 us)
Async XLA Ops:
  0.6 1.5 copy-start
  3.5 2.0 copy-start.14
  21.8 11.3 %collective-permute-start = (f32[4,128,256]{2,1,0:T(8,128)S(1)}, f32[4,128,256]{2,1,0:T(8,128)S(1)}, u32[]{:S(2)}, u32[]{:S(2)}) collective-permute-start(f32[4,128,256]{2,1,0:T(8,128)S(1)} %get-tuple-element.23), channel_id=1, source_target_pairs={{0,1},{1,2},{2,3},{3,4},{4,5},{5,6},{6,7},{7,8},{8,9},{9,10},{10,1... | collective-permute-start | bytes 1572872 | tf_op jit(solution)/shard_map/ppermute | solution.py:13
  26.3 10.8 %collective-permute-start.1 = (f32[4,128,256]{2,1,0:T(8,128)S(1)}, f32[4,128,256]{2,1,0:T(8,128)S(1)}, u32[]{:S(2)}, u32[]{:S(2)}) collective-permute-start(f32[4,128,256]{2,1,0:T(8,128)S(1)} %get-tuple-element.22), channel_id=1, source_target_pairs={{1,0},{2,1},{3,2},{4,3},{5,4},{6,5},{7,6},{8,7},{9,8},{10,9},{11,1... | collective-permute-start | bytes 1572872 | tf_op jit(solution)/shard_map/ppermute | solution.py:13
  28.3 13.9 %collective-permute-start.2 = (f32[4,128,256]{2,1,0:T(8,128)S(1)}, f32[4,128,256]{2,1,0:T(8,128)S(1)}, u32[]{:S(2)}, u32[]{:S(2)}) collective-permute-start(f32[4,128,256]{2,1,0:T(8,128)S(1)} %get-tuple-element.21), channel_id=1, source_target_pairs={{0,32},{32,64},{64,96},{1,33},{33,65},{65,97},{2,34},{34,66},{66,9... | collective-permute-start | bytes 1572872 | tf_op jit(solution)/shard_map/ppermute | solution.py:13
  31.9 14.4 %collective-permute-start.3 = (f32[4,128,256]{2,1,0:T(8,128)S(1)}, f32[4,128,256]{2,1,0:T(8,128)S(1)}, u32[]{:S(2)}, u32[]{:S(2)}) collective-permute-start(f32[4,128,256]{2,1,0:T(8,128)S(1)} %get-tuple-element.20), channel_id=1, source_target_pairs={{32,0},{64,32},{96,64},{33,1},{65,33},{97,65},{34,2},{66,34},{98,6... | collective-permute-start | bytes 1572872 | tf_op jit(solution)/shard_map/ppermute | solution.py:13
  33.2 13.2 %copy-start.7 = (f32[32,128,256]{2,1,0:T(8,128)S(1)}, f32[32,128,256]{2,1,0:T(8,128)}, u32[]{:S(2)}) copy-start(f32[32,128,256]{2,1,0:T(8,128)} %gather_fusion) | copy-start | bytes 12582916
  60.7 13.5 %copy-start.6 = (f32[2,2048,128]{1,2,0:T(8,128)}, f32[2,2048,128]{1,2,0:T(8,128)S(1)}, u32[]{:S(2)}) copy-start(f32[2,2048,128]{1,2,0:T(8,128)S(1)} %copy.142) | copy-start | bytes 6291460
  80.4 14.9 %collective-permute-start.4 = (f32[4,128,128]{2,1,0:T(8,128)}, f32[4,128,128]{2,1,0:T(8,128)S(1)}, u32[]{:S(2)}, u32[]{:S(2)}) collective-permute-start(f32[4,128,128]{2,1,0:T(8,128)} %get-tuple-element.55), channel_id=1, source_target_pairs={{0,1},{1,2},{2,3},{3,4},{4,5},{5,6},{6,7},{7,8},{8,9},{9,10},{10,1... | collective-permute-start | bytes 786440 | tf_op jit(solution)/shard_map/ppermute | solution.py:13
  85.3 10.0 %collective-permute-start.5 = (f32[4,128,128]{2,1,0:T(8,128)}, f32[4,128,128]{2,1,0:T(8,128)S(1)}, u32[]{:S(2)}, u32[]{:S(2)}) collective-permute-start(f32[4,128,128]{2,1,0:T(8,128)} %get-tuple-element.54), channel_id=1, source_target_pairs={{1,0},{2,1},{3,2},{4,3},{5,4},{6,5},{7,6},{8,7},{9,8},{10,9},{11,1... | collective-permute-start | bytes 786440 | tf_op jit(solution)/shard_map/ppermute | solution.py:13
  87.3 8.1 collective-permute-start.6
  90.6 7.9 collective-permute-start.7
  103.8 3.0 copy-start.15
  108.7 1.3 copy-start.4
  110.0 41.0 %copy-start.17 = (f32[12,1536]{1,0:T(8,128)S(1)}, f32[12,1536]{1,0:T(8,128)}, u32[]{:S(2)}) copy-start(f32[12,1536]{1,0:T(8,128)} %param.9) | copy-start | bytes 221188
  158.5 8.7 collective-permute-start.8
  160.7 7.9 collective-permute-start.9
  162.9 8.6 collective-permute-start.10
  165.7 9.5 %collective-permute-start.11 = (f32[4,128,128]{2,1,0:T(8,128)S(1)}, f32[4,128,128]{2,1,0:T(8,128)S(1)}, u32[]{:S(2)}, u32[]{:S(2)}) collective-permute-start(f32[4,128,128]{2,1,0:T(8,128)S(1)} %get-tuple-element.48), channel_id=1, source_target_pairs={{32,0},{64,32},{96,64},{33,1},{65,33},{97,65},{34,2},{66,34},{98,6... | collective-permute-start | bytes 786440 | tf_op jit(solution)/shard_map/ppermute | solution.py:13
  183.6 48.8 %copy-start.2 = (f32[2,2048,128]{1,2,0:T(8,128)}, f32[2,2048,128]{1,2,0:T(8,128)S(1)}, u32[]{:S(2)}) copy-start(f32[2,2048,128]{1,2,0:T(8,128)S(1)} %sub.70) | copy-start | bytes 6291460
  205.7 9.9 %collective-permute-start.12 = (f32[4,128,128]{2,1,0:T(8,128)}, f32[4,128,128]{2,1,0:T(8,128)S(1)}, u32[]{:S(2)}, u32[]{:S(2)}) collective-permute-start(f32[4,128,128]{2,1,0:T(8,128)} %get-tuple-element.47), channel_id=1, source_target_pairs={{0,1},{1,2},{2,3},{3,4},{4,5},{5,6},{6,7},{7,8},{8,9},{9,10},{10,1... | collective-permute-start | bytes 786440 | tf_op jit(solution)/shard_map/ppermute | solution.py:13
  209.8 14.4 %copy-start.8 = (f32[32,128,128]{2,1,0:T(8,128)S(1)}, f32[32,128,128]{2,1,0:T(8,128)}, u32[]{:S(2)}) copy-start(f32[32,128,128]{2,1,0:T(8,128)} %gather_fusion.7) | copy-start | bytes 6291460
  209.8 10.7 %collective-permute-start.14 = (f32[4,128,128]{2,1,0:T(8,128)S(1)}, f32[4,128,128]{2,1,0:T(8,128)S(1)}, u32[]{:S(2)}, u32[]{:S(2)}) collective-permute-start(f32[4,128,128]{2,1,0:T(8,128)S(1)} %get-tuple-element.45), channel_id=1, source_target_pairs={{0,32},{32,64},{64,96},{1,33},{33,65},{65,97},{2,34},{34,66},{66,9... | collective-permute-start | bytes 786440 | tf_op jit(solution)/shard_map/ppermute | solution.py:13
  212.3 8.2 collective-permute-start.13
  214.3 9.9 %collective-permute-start.15 = (f32[4,128,128]{2,1,0:T(8,128)S(1)}, f32[4,128,128]{2,1,0:T(8,128)S(1)}, u32[]{:S(2)}, u32[]{:S(2)}) collective-permute-start(f32[4,128,128]{2,1,0:T(8,128)S(1)} %get-tuple-element.44), channel_id=1, source_target_pairs={{32,0},{64,32},{96,64},{33,1},{65,33},{97,65},{34,2},{66,34},{98,6... | collective-permute-start | bytes 786440 | tf_op jit(solution)/shard_map/ppermute | solution.py:13
  302.0 81.0 %copy-start.5 = (f32[2,2048,128]{1,2,0:T(8,128)}, f32[2,2048,128]{1,2,0:T(8,128)S(1)}, u32[]{:S(2)}) copy-start(f32[2,2048,128]{1,2,0:T(8,128)S(1)} %multiply_subtract_fusion.2) | copy-start | bytes 6291460
  355.4 19.5 %copy-start.10 = (f32[32,128,128]{2,1,0:T(8,128)S(1)}, f32[32,128,128]{2,1,0:T(8,128)}, u32[]{:S(2)}) copy-start(f32[32,128,128]{2,1,0:T(8,128)} %gather_fusion.9) | copy-start | bytes 6291460
  356.8 9.2 collective-permute-start.16
  359.5 7.7 collective-permute-start.17
  361.5 9.2 collective-permute-start.18
  364.7 10.1 %collective-permute-start.19 = (f32[4,128,128]{2,1,0:T(8,128)S(1)}, f32[4,128,128]{2,1,0:T(8,128)S(1)}, u32[]{:S(2)}, u32[]{:S(2)}) collective-permute-start(f32[4,128,128]{2,1,0:T(8,128)S(1)} %get-tuple-element.40), channel_id=1, source_target_pairs={{32,0},{64,32},{96,64},{33,1},{65,33},{97,65},{34,2},{66,34},{98,6... | collective-permute-start | bytes 786440 | tf_op jit(solution)/shard_map/ppermute | solution.py:13
  471.0 19.4 %copy-start.11 = (f32[32,128,128]{2,1,0:T(8,128)S(1)}, f32[32,128,128]{2,1,0:T(8,128)}, u32[]{:S(2)}) copy-start(f32[32,128,128]{2,1,0:T(8,128)} %gather_fusion.11) | copy-start | bytes 6291460
  472.5 9.1 collective-permute-start.20
  475.7 7.7 collective-permute-start.21
  477.6 8.6 collective-permute-start.22
  480.2 10.1 %collective-permute-start.23 = (f32[4,128,128]{2,1,0:T(8,128)S(1)}, f32[4,128,128]{2,1,0:T(8,128)S(1)}, u32[]{:S(2)}, u32[]{:S(2)}) collective-permute-start(f32[4,128,128]{2,1,0:T(8,128)S(1)} %get-tuple-element.36), channel_id=1, source_target_pairs={{32,0},{64,32},{96,64},{33,1},{65,33},{97,65},{34,2},{66,34},{98,6... | collective-permute-start | bytes 786440 | tf_op jit(solution)/shard_map/ppermute | solution.py:13
  566.4 1.3 copy-start.3
  621.4 19.1 %copy-start.12 = (f32[32,128,128]{2,1,0:T(8,128)S(1)}, f32[32,128,128]{2,1,0:T(8,128)}, u32[]{:S(2)}) copy-start(f32[32,128,128]{2,1,0:T(8,128)} %gather_fusion.13) | copy-start | bytes 6291460
  622.9 8.8 collective-permute-start.24
  625.6 7.7 collective-permute-start.25
  627.6 8.9 collective-permute-start.26
  630.4 10.1 %collective-permute-start.27 = (f32[4,128,128]{2,1,0:T(8,128)S(1)}, f32[4,128,128]{2,1,0:T(8,128)S(1)}, u32[]{:S(2)}, u32[]{:S(2)}) collective-permute-start(f32[4,128,128]{2,1,0:T(8,128)S(1)} %get-tuple-element.32), channel_id=1, source_target_pairs={{32,0},{64,32},{96,64},{33,1},{65,33},{97,65},{34,2},{66,34},{98,6... | collective-permute-start | bytes 786440 | tf_op jit(solution)/shard_map/ppermute | solution.py:13
  735.9 19.3 %copy-start.13 = (f32[32,128,128]{2,1,0:T(8,128)S(1)}, f32[32,128,128]{2,1,0:T(8,128)}, u32[]{:S(2)}) copy-start(f32[32,128,128]{2,1,0:T(8,128)} %gather_fusion.15) | copy-start | bytes 6291460
  737.3 9.0 collective-permute-start.28
  740.3 7.7 collective-permute-start.29
  742.2 8.8 collective-permute-start.30
  745.1 10.1 %collective-permute-start.31 = (f32[4,128,128]{2,1,0:T(8,128)S(1)}, f32[4,128,128]{2,1,0:T(8,128)S(1)}, u32[]{:S(2)}, u32[]{:S(2)}) collective-permute-start(f32[4,128,128]{2,1,0:T(8,128)S(1)} %get-tuple-element.28), channel_id=1, source_target_pairs={{32,0},{64,32},{96,64},{33,1},{65,33},{97,65},{34,2},{66,34},{98,6... | collective-permute-start | bytes 786440 | tf_op jit(solution)/shard_map/ppermute | solution.py:13
  885.7 19.6 %copy-start.9 = (f32[32,128,128]{2,1,0:T(8,128)S(1)}, f32[32,128,128]{2,1,0:T(8,128)}, u32[]{:S(2)}) copy-start(f32[32,128,128]{2,1,0:T(8,128)} %gather_fusion.17) | copy-start | bytes 6291460
  887.2 9.3 collective-permute-start.32
  889.7 7.7 collective-permute-start.33
  891.6 9.5 %collective-permute-start.34 = (f32[4,128,128]{2,1,0:T(8,128)S(1)}, f32[4,128,128]{2,1,0:T(8,128)S(1)}, u32[]{:S(2)}, u32[]{:S(2)}) collective-permute-start(f32[4,128,128]{2,1,0:T(8,128)S(1)} %get-tuple-element.25), channel_id=1, source_target_pairs={{0,32},{32,64},{64,96},{1,33},{33,65},{65,97},{2,34},{34,66},{66,9... | collective-permute-start | bytes 786440 | tf_op jit(solution)/shard_map/ppermute | solution.py:13
  895.1 10.1 %collective-permute-start.35 = (f32[4,128,128]{2,1,0:T(8,128)S(1)}, f32[4,128,128]{2,1,0:T(8,128)S(1)}, u32[]{:S(2)}, u32[]{:S(2)}) collective-permute-start(f32[4,128,128]{2,1,0:T(8,128)S(1)} %get-tuple-element.24), channel_id=1, source_target_pairs={{32,0},{64,32},{96,64},{33,1},{65,33},{97,65},{34,2},{66,34},{98,6... | collective-permute-start | bytes 786440 | tf_op jit(solution)/shard_map/ppermute | solution.py:13
  922.3 3.0 copy-start.16
  925.3 1.8 copy-start.1
where the time goes:
time: 938 us; the launch traced here: 927 us
  blocking collectives  471 us (50%)
  local copies, waits for them, and re-layouts  155 us (17%)
  starting transfers between devices  86.1 us (9%)
  matrix products  83.3 us (9%)
  waiting for transfers between devices  76.1 us (8%)
  other arithmetic  54.6 us (6%)
    psum x3, blocking collectives, residual_norm(): return lax.psum(inner_product(values, values), ('cluster', 'sub'))  191 us
    all_gather x4, blocking collectives, coarse_coefficients(): lax.all_gather(coarse_terms, ('cluster', 'sub'), axis=0, tiled=True)  153 us
    psum x2, blocking collectives, on_device(): lax.psum(inner_product(direction, image_dir), ('cluster', 'sub'))  127 us
    ppermute x36, starting transfers between devices, from_behind(): lax.ppermute(value, axis, [(source, source + steps) for source in range(i...  86.1 us
    ppermute x36, waiting for transfers between devices, from_behind(): lax.ppermute(value, axis, [(source, source + steps) for source in range(i...  76.1 us
    dot_general x4, matrix products, apply_dual(): jnp.einsum('smn,snl->sml', dual_operators, direction.astype(jnp.bfloat16)...  53.1 us
    gather x9, local copies, waits for them, and re-layouts, from_slots(): slot_values[inverse].reshape(local_count, dual_order, slot_values.shape[-1])  32.8 us
    gather x9, local copies, waits for them, and re-layouts, to_slots(): return values.reshape(block_total, block_size, values.shape[-1])[slot_order]  31.2 us
  transfers between devices with their start and end apart: 36, of which 24 were waited for; matrix products, arithmetic and copies ran while one was open for 0% of the time, Pallas kernels for 0%

commit v1 on v0

v1 whole, which is shorter than its diff:
```python
import jax
import jax.numpy as jnp
from jax import lax
from jax.experimental import pallas as pl
from jax.experimental.pallas import tpu as pltpu
from jax.sharding import PartitionSpec as P

NMODE = 6
ITERS = 3
BLK = 128
GRP = 16
NGRP = 5
ROWS = GRP * NGRP
F32, BF16 = jnp.float32, jnp.bfloat16
HIGHEST = lax.Precision.HIGHEST


def dot(a, b):
    return jnp.dot(a, b, preferred_element_type=F32)


def split(x):
    hi = x.astype(BF16)
    return hi, (x - hi.astype(F32)).astype(BF16)


def stacked(a):
    hi, lo = split(a)
    return jnp.concatenate([hi, hi, lo, jnp.zeros((256 - 3 * ROWS, a.shape[1]), BF16)], axis=0)


def params(mib):
    return pltpu.CompilerParams(dimension_semantics=("arbitrary",), vmem_limit_bytes=mib << 20)


def whole(shape):
    return pl.BlockSpec(shape, lambda *_: (0,) * len(shape))


def shape(dims, dtype=F32):
    return jax.ShapeDtypeStruct(dims, dtype)


def prep_body(slot, modes, coarse, rs, p0, p1, p2, p3):
    payloads = (p0, p1, p2, p3)
    nc = coarse.shape[1]
    for p in payloads:
        p[0:12, 0:nc] = coarse[...]
        p[12:16, 0:nc] = jnp.zeros((4, nc), F32)
    for s in range(32):
        b = slot[s]
        t, j = b // 16, b % 16
        at = pl.ds(pl.multiple_of(j * BLK, BLK), BLK)
        rs[s] = jnp.zeros((GRP, BLK), F32)
        rs[s, 0:6, :] = jnp.where(t == 0, modes[0, :, at], 0.0)
        rs[s, 6:12, :] = jnp.where(t == 1, modes[1, :, at], 0.0)
        if s < 16:
            payloads[s // 4][:, nc + (s % 4) * BLK : nc + (s % 4 + 1) * BLK] = rs[s]


def prep(slot, modes, coarse):
    nc = coarse.shape[1]
    return pl.pallas_call(
        prep_body,
        grid_spec=pltpu.PrefetchScalarGridSpec(
            num_scalar_prefetch=1,
            grid=(1,),
            in_specs=[whole(modes.shape), whole(coarse.shape)],
            out_specs=[whole((32, GRP, BLK))] + [whole((GRP, nc + 4 * BLK))] * 4,
        ),
        out_shape=[shape((32, GRP, BLK))] + [shape((GRP, nc + 4 * BLK))] * 4,
        compiler_params=params(16),
    )(slot, modes, coarse)


def init_body(slot, wm, rs, q0, q1, q2, q3, coarse, loads, bcat, bt2, c2, lam, xb, c60, bt):
    received = (q0, q1, q2, q3)
    nc = coarse.shape[1]
    c60[...] = jnp.zeros(c60.shape, F32)
    c60[0:12, :] = coarse[...]
    for g in range(4):
        c60[GRP * (g + 1) : GRP * (g + 2), :] = received[g][:, 0:nc]
    hi, lo = split(c60[...])
    c2[0:ROWS, :] = hi
    c2[ROWS:, :] = lo
    a = jnp.dot(c60[...], loads[...], precision=HIGHEST, preferred_element_type=F32)
    acat = stacked(a)
    for s in range(32):
        f, k = s // 4, s % 4
        bt[...] = jnp.zeros(bt.shape, F32)
        own = rs[s]
        if f >= 6:
            own = own - rs[s + 4 if f == 6 else s - 4]
        bt[0:GRP, :] = own
        if f < 4:
            bt[GRP * (f + 1) : GRP * (f + 2), :] = -wm[8 + f] * received[f][:, nc + k * BLK : nc + (k + 1) * BLK]
        v = bt[...]
        vh = v.astype(BF16)
        vhf = vh.astype(F32)
        vl = v - vhf
        bt2[s, 0:ROWS, :] = vh
        bt2[s, ROWS:, :] = vl.astype(BF16)
        tall = jnp.concatenate([vhf, vl, vhf, jnp.zeros((256 - 3 * ROWS, BLK), F32)], axis=0)
        wide = tall.T.astype(BF16)
        bcat[s] = wide
        x = dot(wide, acat)
        lam[s] = x
        xb[slot[s]] = x.astype(BF16)


def initial(slot, wm, rs, received, coarse, coarse_loads):
    nc = coarse.shape[1]
    args = (rs, *received, coarse, coarse_loads)
    outs = [
        shape((32, BLK, 256), BF16),
        shape((32, 2 * ROWS, BLK), BF16),
        shape((2 * ROWS, nc), BF16),
        shape((32, BLK, BLK)),
        shape((32, BLK, BLK), BF16),
    ]
    return pl.pallas_call(
        init_body,
        grid_spec=pltpu.PrefetchScalarGridSpec(
            num_scalar_prefetch=2,
            grid=(1,),
            in_specs=[whole(x.shape) for x in args],
            out_specs=[whole(x.shape) for x in outs],
            scratch_shapes=[pltpu.VMEM((ROWS, nc), F32), pltpu.VMEM((ROWS, BLK), F32)],
        ),
        out_shape=outs,
        compiler_params=params(32),
    )(slot, wm, *args)


def apply_body(first, inv, k_ref, x_ref, bt2, *refs):
    if first:
        loads, y, y0, y1, y2, y3, eo, el, er, ed, eu, acc, dacc = refs
    else:
        u0, u1, u2, u3, part, y, y0, y1, y2, y3, eo, el, er, ed, eu, acc, dacc = refs
        us = (u0, u1, u2, u3)
    i = pl.program_id(0)

    @pl.when(i == 0)
    def _():
        acc[...] = jnp.zeros(acc.shape, F32)
        dacc[...] = jnp.zeros(dacc.shape, F32)

    tile = dot(k_ref[0], x_ref[0])
    total = acc[...]
    delta = dacc[...]
    for j in range(4):
        s = inv[4 * i + j]
        yb = tile[j * BLK : (j + 1) * BLK]
        if first:
            yb = loads[j] - yb
        else:
            delta = delta + jnp.sum((us[j][0] * yb).reshape(16, 8, BLK), axis=0)
        y[s] = yb
        hi, lo = split(yb)
        both = dot(bt2[s], hi)
        total = total + (both[:ROWS] + both[ROWS:]) + dot(bt2[s, 0:ROWS, :], lo)
    acc[...] = total
    dacc[...] = delta

    @pl.when(i == pl.num_programs(0) - 1)
    def _():
        for f, out in enumerate((y0, y1, y2, y3)):
            out[...] = y[4 * f : 4 * f + 4]
        own = acc[0:GRP, :]
        if not first:
            rows = lax.broadcasted_iota(jnp.int32, (GRP, BLK), 0)
            own = jnp.where(rows == 12, jnp.sum(dacc[...], axis=0, keepdims=True), own)
            own = jnp.where(rows == 13, part[0:1, :], own)
            own = jnp.where(rows == 14, part[1:2, :], own)
        eo[...] = own
        for g, out in enumerate((el, er, ed, eu)):
            out[...] = acc[GRP * (g + 1) : GRP * (g + 2), :]


def apply_dual(inv, k, xb, bt2, loads=None, u=None, part=None):
    first = loads is not None
    order = k.shape[1]
    tiles = order // 512
    args = [k, xb.reshape(k.shape[0], order, BLK), bt2]
    specs = [
        pl.BlockSpec((1, 512, order), lambda i, inv: (i // tiles, i % tiles, 0)),
        pl.BlockSpec((1, order, BLK), lambda i, inv: (i // tiles, 0, 0)),
        whole(bt2.shape),
    ]
    if first:
        args.append(loads.reshape(32, BLK, BLK))
        specs.append(pl.BlockSpec((4, BLK, BLK), lambda i, inv: (i, 0, 0)))
    else:
        for j in range(4):
            args.append(u)
            specs.append(pl.BlockSpec((1, BLK, BLK), lambda i, inv, j=j: (inv[4 * i + j], 0, 0)))
        args.append(part)
        specs.append(whole(part.shape))
    outs = [shape((32, BLK, BLK))] + [shape((4, BLK, BLK))] * 4 + [shape((GRP, BLK))] * 5
    return pl.pallas_call(
        lambda *refs: apply_body(first, *refs),
        grid_spec=pltpu.PrefetchScalarGridSpec(
            num_scalar_prefetch=1,
            grid=(8,),
            in_specs=specs,
            out_specs=[whole(x.shape) for x in outs],
            scratch_shapes=[pltpu.VMEM((ROWS, BLK), F32), pltpu.VMEM((8, BLK), F32)],
        ),
        out_shape=outs,
        compiler_params=params(24),
        name="apply_first" if first else "apply",
    )(inv, *args)


def update_body(kind, slot, tab, wm, *refs):
    first, last, chained = kind == 0, kind == ITERS, kind >= 2
    refs = list(refs)
    take = lambda n: [refs.pop(0) for _ in range(n)]
    h, c2, r0, r1, r2, r3, y, yp, bcat = take(9)
    if not first:
        (u,) = take(1)
    if chained:
        img_in, a_in, scal_in = take(3)
    if last:
        lam_in, d_in = take(2)
        lam_out, u_out = take(2)
    elif first:
        u_out, xb, part = take(3)
    else:
        u_out, xb, part, img_out, a_out, scal = take(6)
    habs, acat, pr, coef, sums = take(5)
    f = pl.program_id(0)

    @pl.when(f == 0)
    def _():
        tail = jnp.zeros((8, BLK), F32)
        for j in range(128):
            piece = h[tab[j]]
            habs[12 * j : 12 * j + 12, :] = piece[0:12]
            tail = tail + piece[8:16]
        hi, lo = split(habs[...])
        both = dot(c2[...], hi)
        a = both[:ROWS] + both[ROWS:] + dot(c2[0:ROWS, :], lo)
        sums[...] = jnp.zeros(sums.shape, F32)
        if not first:
            delta, gamma, eps = tail[4:5], tail[5:6], tail[6:7]
            if chained:
                beta = gamma / scal_in[0:1, :]
                curve = delta + 2.0 * beta * eps + beta * beta * scal_in[1:2, :]
                a = a + beta * a_in[...]
                coef[1:2, :] = beta
            else:
                curve = delta
            step = gamma / curve
            coef[0:1, :] = step
            if not last:
                a_out[...] = a
                scal[...] = jnp.zeros(scal.shape, F32)
                scal[0:1, :] = gamma
                scal[1:2, :] = curve
                scal[2:3, :] = step
                if chained:
                    scal[3:4, :] = beta
        acat[...] = stacked(a)

    for g, r in enumerate((r0, r1, r2, r3)):

        @pl.when(f == g)
        def _():
            pr[...] = r[...] * wm[8 + g]

    @pl.when((f == 4) | (f == 5))
    def _():
        pr[...] = jnp.zeros(pr.shape, F32)

    @pl.when(f >= 6)
    def _():
        pr[...] = yp[...]

    w = wm[f]
    for k in range(4):
        image = y[k] - pr[k]
        if chained:
            image = image + coef[1:2, :] * img_in[k]
        fix = dot(bcat[k], acat[...])
        if first:
            new = image - fix
        else:
            new = u[k] - coef[0:1, :] * (image - fix)
        b = slot[4 * f + k]
        if last:
            direction = u[k] + coef[1:2, :] * d_in[k]
            lam_out[b] = lam_in[k] + coef[0:1, :] * direction
            u_out[b] = new
        else:
            u_out[k] = new
            xb[b] = new.astype(BF16)
            weighted = new * w
            sums[0:8, :] += jnp.sum((weighted * new).reshape(16, 8, BLK), axis=0)
            if not first:
                img_out[k] = image
                sums[8:16, :] += jnp.sum((weighted * image).reshape(16, 8, BLK), axis=0)

    if not last:

        @pl.when(f == pl.num_programs(0) - 1)
        def _():
            part[...] = jnp.zeros(part.shape, F32)
            part[0:1, :] = jnp.sum(sums[0:8, :], axis=0, keepdims=True)
            part[1:2, :] = jnp.sum(sums[8:16, :], axis=0, keepdims=True)


def update(kind, slot, tab, wm, h, c2, received, y, bcat, u=None, chain=None, closing=None):
    first, last, chained = kind == 0, kind == ITERS, kind >= 2
    face = pl.BlockSpec((4, BLK, BLK), lambda f, *_: (f, 0, 0))
    args = [h, c2, *received, y, y, bcat]
    specs = [whole(x.shape) for x in args[:6]]
    specs += [
        face,
        pl.BlockSpec((4, BLK, BLK), lambda f, *_: (jnp.where(f >= 6, 13 - f, 7), 0, 0)),
        pl.BlockSpec((4, BLK, 256), lambda f, *_: (f, 0, 0)),
    ]
    if not first:
        args.append(u)
        specs.append(face)
    if chained:
        args += list(chain)
        specs += [face, whole(chain[1].shape), whole(chain[2].shape)]
    vector, small = shape((32, BLK, BLK)), shape((8, BLK))
    if last:
        args += list(closing)
        specs += [face, face]
        outs, out_specs = [vector, vector], [whole(vector.shape)] * 2
    else:
        outs = [vector, shape((32, BLK, BLK), BF16), small]
        out_specs = [face, whole(vector.shape), whole(small.shape)]
        if not first:
            outs += [vector, shape((ROWS, BLK)), small]
            out_specs += [face, whole((ROWS, BLK)), whole(small.shape)]
    return pl.pallas_call(
        lambda *refs: update_body(kind, *refs),
        grid_spec=pltpu.PrefetchScalarGridSpec(
            num_scalar_prefetch=3,
            grid=(8,),
            in_specs=specs,
            out_specs=out_specs,
            scratch_shapes=[
                pltpu.VMEM((c2.shape[1], BLK), F32),
                pltpu.VMEM((256, BLK), BF16),
                pltpu.VMEM((4, BLK, BLK), F32),
                pltpu.VMEM((8, BLK), F32),
                pltpu.VMEM((16, BLK), F32),
            ],
        ),
        out_shape=outs,
        compiler_params=params(24),
        name=f"update_{kind}",
    )(slot, tab, wm, *args)


def on_device(dual_operators, local_loads, modes, coarse_matrix, coarse_loads, slot_block):
    n_sub, n_cluster = lax.axis_size("sub"), lax.axis_size("cluster")
    own, cluster = lax.axis_index("sub"), lax.axis_index("cluster")
    slot = slot_block[0]
    positions = jnp.arange(32, dtype=jnp.int32)
    inv = jnp.sum(positions[:, None] * (slot[:, None] == positions[None, :]).astype(jnp.int32), axis=0)
    there = jnp.stack([own > 0, own < n_sub - 1, cluster > 0, cluster < n_cluster - 1])
    one = jnp.ones((4,), F32)
    wm = jnp.concatenate([jnp.where(there, 0.5, 1.0), jnp.array([1.0, 1.0, 0.5, 0.5]), there.astype(F32), one]).astype(F32)

    device = jnp.arange(n_sub * n_cluster, dtype=jnp.int32)
    dz, dsub = device // n_sub, device % n_sub
    far = lambda now, mine: (now - mine) % 4
    tab = (
        (((dsub % 2) ^ (own % 2)) * 4 + far(dsub // 2 % 4, own // 2 % 4)) * 4 + far(dsub // 8, own // 8)
    ) * 4 + far(dz, cluster)

    def along_sub(value, source):
        return lax.ppermute(value, "sub", [(source(i), i) for i in range(n_sub)])

    def along_cluster(value, k):
        return lax.ppermute(value, "cluster", [((i + k) % n_cluster, i) for i in range(n_cluster)])

    def exchange(p0, p1, p2, p3):
        return [
            along_sub(p1, lambda i: (i - 1) % n_sub),
            along_sub(p0, lambda i: (i + 1) % n_sub),
            along_cluster(p3, -1),
            along_cluster(p2, 1),
        ]

    def gather(faces, groups):
        eo, el, er, ed, eu = groups
        mine = eo + along_sub(er, lambda i: (i - 1) % n_sub) + along_sub(el, lambda i: (i + 1) % n_sub)
        sent = lax.optimization_barrier(jnp.concatenate([mine, ed, eu], axis=0))
        z = [sent] + [along_cluster(sent, k) for k in (1, 2, 3)]
        z, faces = lax.optimization_barrier((z, faces))
        received = exchange(*faces)
        h = [z[k][:GRP] + z[(k + 1) % 4][GRP : 2 * GRP] + z[(k + 3) % 4][2 * GRP :] for k in range(4)]
        h = lax.optimization_barrier(jnp.concatenate(h, axis=0))
        for step in (8, 2):
            place = lambda i, k: i - i % (4 * step) + (i + k * step) % (4 * step)
            h = [h] + [along_sub(h, lambda i, k=k: place(i, k)) for k in (1, 2, 3)]
            h = lax.optimization_barrier(jnp.concatenate(h, axis=0))
        h = jnp.concatenate([h, along_sub(h, lambda i: i ^ 1)], axis=0)
        return h.reshape(128, GRP, BLK), received

    rs, *payload = prep(slot, modes, coarse_matrix)
    neighbours = exchange(*payload)
    bcat, bt2, c2, lam, xb = initial(slot, wm, rs, neighbours, coarse_matrix, coarse_loads)

    y, *sent = apply_dual(inv, dual_operators, xb, bt2, loads=local_loads)
    h, received = gather(sent[:4], sent[4:])
    u, xb, part = update(0, slot, tab, wm, h, c2, received, y, bcat)
    chain, direction = None, None
    for kind in range(1, ITERS + 1):
        y, *sent = apply_dual(inv, dual_operators, xb, bt2, u=u, part=part)
        h, received = gather(sent[:4], sent[4:])
        closing = (lam, direction) if kind == ITERS else None
        outs = update(kind, slot, tab, wm, h, c2, received, y, bcat, u, chain, closing)
        if kind < ITERS:
            new, xb, part, image, a, scal = outs
            direction = u if direction is None else u + scal[3] * direction
            lam = lam + scal[2] * direction
            u, chain = new, (image, a, scal)
    shape_out = local_loads.shape
    return outs[0].reshape(shape_out), outs[1].reshape(shape_out)


def solution(mesh):
    spec = P(("cluster", "sub"), None, None)
    flat = P(("cluster", "sub"), None)
    return jax.shard_map(
        on_device,
        mesh=mesh,
        in_specs=(spec, spec, spec, flat, P(), flat),
        out_specs=(spec, spec),
        check_vma=False,
    )
```

time: 938 us -> 282 us (0.30)
  blocking collectives: 471 us -> 0 us
  local copies, waits for them, and re-layouts: 155 us -> 33.2 us
  matrix products: 83.3 us -> 0 us
  Pallas kernels: 0 us -> 53.6 us
  other arithmetic: 54.6 us -> 6.61 us
  starting transfers between devices: 86.1 us -> 106 us
    psum x5 -> x0, blocking collectives: 317 us -> none  [the longest x3 191 us: residual_norm(): return lax.psum(inner_product(values, values), ('cluster', 'sub'))]
    all_gather x4 -> x0, blocking collectives: 153 us -> none  [coarse_coefficients(): lax.all_gather(coarse_terms, ('cluster', 'sub'), axis=0, tiled=True)]
    dot_general x18 -> x0, matrix products: 83.3 us -> none  [the longest x4 53.1 us: apply_dual(): jnp.einsum('smn,snl->sml', dual_operators, direction.astype(jnp.bfloat16)...]
    gather x19 -> x0, local copies, waits for them, and re-layouts: 64.7 us -> none  [the longest x9 32.8 us: from_slots(): slot_values[inverse].reshape(local_count, dual_order, slot_values.shape[-1])]
    pallas_call x0 -> x10, Pallas kernels: none -> 53.6 us  [the longest x4 35.5 us: apply_dual(): pl.pallas_call(lambda *refs: apply_body(first, *refs), grid_spec=pltpu.Pr...]
    sub x14 -> x0, other arithmetic: 33.8 us -> none  [the longest x9 15.5 us: assemble(): return from_slots(sent - receive(sent))]
    dot_general x8 -> x0, local copies, waits for them, and re-layouts: 22.4 us -> none  [the longest x4 11.7 us: apply_dual(): jnp.einsum('smn,snl->sml', dual_operators, direction.astype(jnp.bfloat16)...]
    reshape x13 -> x0, local copies, waits for them, and re-layouts: 22.2 us -> none  [the longest x8 22.2 us: from_slots(): slot_values[inverse].reshape(local_count, dual_order, slot_values.shape[-1])]
  transfers between devices with their start and end apart: 36 -> 68, of which waited for: 24 -> 49; matrix products, arithmetic and copies ran while one was open for 0% -> 2% of each run, Pallas kernels for 0% -> 0%
where the time goes in v1:
time: 282 us; the launch traced here: 277 us
  starting transfers between devices  106 us (38%)
  waiting for transfers between devices  76.8 us (27%)
  Pallas kernels  53.6 us (19%)
  local copies, waits for them, and re-layouts  33.2 us (12%)
  other arithmetic  6.61 us (2%)
    ppermute x46, starting transfers between devices, along_sub(): return lax.ppermute(value, 'sub', [(source(i), i) for i in range(n_sub)])  77.5 us
    ppermute x46, waiting for transfers between devices, along_sub(): return lax.ppermute(value, 'sub', [(source(i), i) for i in range(n_sub)])  58.4 us
    pallas_call x4, Pallas kernels, apply_dual(): pl.pallas_call(lambda *refs: apply_body(first, *refs), grid_spec=pltpu.Pr...  35.5 us
    unnamed x89, local copies, waits for them, and re-layouts  33.2 us
    ppermute x22, starting transfers between devices, along_cluster(): lax.ppermute(value, 'cluster', [((i + k) % n_cluster, i) for i in range(n...  28.2 us
    ppermute x22, waiting for transfers between devices, along_cluster(): lax.ppermute(value, 'cluster', [((i + k) % n_cluster, i) for i in range(n...  18.5 us
    pallas_call x4, Pallas kernels, update(): pl.pallas_call(lambda *refs: update_body(kind, *refs), grid_spec=pltpu.Pr...  15.4 us
  transfers between devices with their start and end apart: 68, of which 49 were waited for; matrix products, arithmetic and copies ran while one was open for 2% of the time, Pallas kernels for 0%

profile of v1, /device:TPU:1, one launch (start us, length us, event | category | flops | bytes accessed | tf_op | source)
XLA Modules:
  0.0 277.1 jit_solution(18354662028932772343)
XLA Ops:
  4.7 2.6 collective-permute-start
  7.3 1.6 collective-permute-start.2
  8.9 2.1 collective-permute-start.3
  21.0 1.9 shard_map.87
  23.7 1.3 copy-done.19
  25.1 6.3 %copy-done = bf16[2,2048,2048]{2,1,0:T(8,128)(2,1)S(1)} copy-done((bf16[2,2048,2048]{2,1,0:T(8,128)(2,1)S(1)}, bf16[2,2048,2048]{2,1,0:T(8,128)(2,1)}, u32[]{:S(2)}) %copy-start) | copy-done | bytes 16777240
  31.4 1.6 copy-done.18
  33.0 8.7 %apply_first.1 = (f32[32,128,128]{2,1,0:T(8,128)S(1)}, f32[4,128,128]{2,1,0:T(8,128)S(1)}, f32[4,128,128]{2,1,0:T(8,128)S(1)}, f32[4,128,128]{2,1,0:T(8,128)S(1)...) custom-call(s32[32]{0:T(128)S(1)} %select_reduce_fusion.refs_0_, ...), custom_call_target="tpu_custom_call" | custom-call | tf_op jit(solution)/shard_map/apply_first/pallas_call | solution.py:200
  41.6 1.3 copy-done.13
  44.4 3.2 %collective-permute-start.4 = (f32[16,128]{1,0:T(8,128)S(1)}, f32[16,128]{1,0:T(8,128)S(1)}, u32[]{:S(2)}, u32[]{:S(2)}) collective-permute-start(f32[16,128]{1,0:T(8,128)S(1)} %get-tuple-element.109), channel_id=1, source_target_pairs={{31,0},{0,1},{1,2},{2,3},{3,4},{4,5},{5,6},{6,7},{7,8},{8,9},{9,10... | collective-permute-start | bytes 24584 | tf_op jit(solution)/shard_map/ppermute | solution.py:379
  47.5 1.7 collective-permute-start.5
  50.6 2.1 collective-permute-start.6
  53.7 3.3 %collective-permute-done.7 = f32[48,128]{1,0:T(8,128)S(1)} collective-permute-done((f32[48,128]{1,0:T(8,128)S(1)}, f32[48,128]{1,0:T(8,128)S(1)}, u32[]{:S(2)}, u32[]{:S(2)}) %collective-permute-start.7) | collective-permute-done | bytes 24608 | tf_op jit(solution)/shard_map/ppermute | solution.py:382
  57.0 3.0 %collective-permute-start.10 = (f32[64,128]{1,0:T(8,128)S(1)}, f32[64,128]{1,0:T(8,128)S(1)}, u32[]{:S(2)}, u32[]{:S(2)}) collective-permute-start(f32[64,128]{1,0:T(8,128)S(1)} %pad_maximum_fusion.12), channel_id=1, source_target_pairs={{16,0},{17,1},{18,2},{19,3},{20,4},{21,5},{22,6},{23,7},{24,8},{25... | collective-permute-start | bytes 98312 | tf_op jit(solution)/shard_map/ppermute | solution.py:379
  60.4 2.3 collective-permute-start.9
  62.7 1.3 collective-permute-done.11
  64.0 6.9 %collective-permute-start.12 = (f32[256,128]{1,0:T(8,128)S(1)}, f32[256,128]{1,0:T(8,128)S(1)}, u32[]{:S(2)}, u32[]{:S(2)}) collective-permute-start(f32[256,128]{1,0:T(8,128)S(1)} %pad_maximum_fusion.8), channel_id=1, source_target_pairs={{2,0},{3,1},{4,2},{5,3},{6,4},{7,5},{0,6},{1,7},{10,8},{11,9},{12,... | collective-permute-start | bytes 393224 | tf_op jit(solution)/shard_map/ppermute | solution.py:379
  71.6 4.8 %collective-permute-done.12 = f32[256,128]{1,0:T(8,128)S(1)} collective-permute-done((f32[256,128]{1,0:T(8,128)S(1)}, f32[256,128]{1,0:T(8,128)S(1)}, u32[]{:S(2)}, u32[]{:S(2)}) %collective-permute-start.12) | collective-permute-done | bytes 131104 | tf_op jit(solution)/shard_map/ppermute | solution.py:379
  77.7 2.7 collective-permute-done.14
  82.2 2.7 collective-permute-start.19
  86.2 1.8 collective-permute-done.17.refs_6_
  90.2 3.2 %update_0.1 = (f32[32,128,128]{2,1,0:T(8,128)S(1)}, bf16[32,128,128]{2,1,0:T(8,128)(2,1)S(1)}, f32[8,128]{1,0:T(8,128)S(1)}) custom-call(s32[32]{0:T(128)S(1)} %bitcast.36, s32[128]{0:T(128)S(1)} %fusion.2.refs_1_, f32[16]{0:T(128)S(1)} %pad_maximum_fusion.20.wm.refs_2_, f32[128,16,128]{2,1,0:T(8,128)S(1)} %bitcast.26, bf16[160,1536]{1,0:T(8,128)(2,1)S(1)} %copy-done.16, ...), custom_call_target="tpu_custom_call" | custom-call | tf_op jit(solution)/shard_map/update_0/pallas_call | solution.py:340
  93.4 6.5 %copy-done.1 = bf16[2,2048,2048]{2,1,0:T(8,128)(2,1)S(1)} copy-done((bf16[2,2048,2048]{2,1,0:T(8,128)(2,1)S(1)}, bf16[2,2048,2048]{2,1,0:T(8,128)(2,1)}, u32[]{:S(2)}) %copy-start.1) | copy-done | bytes 16777240
  99.9 8.6 %apply.3 = (f32[32,128,128]{2,1,0:T(8,128)S(1)}, f32[4,128,128]{2,1,0:T(8,128)S(1)}, f32[4,128,128]{2,1,0:T(8,128)S(1)}, f32[4,128,128]{2,1,0:T(8,128)S(1)}, f32...) custom-call(s32[32]{0:T(128)S(1)} %select_reduce_fusion.refs_0_, ...), custom_call_target="tpu_custom_call" | custom-call | tf_op jit(solution)/shard_map/apply/pallas_call | solution.py:200
  108.6 2.3 collective-permute-start.20
  110.9 3.4 %collective-permute-start.21 = (f32[16,128]{1,0:T(8,128)S(1)}, f32[16,128]{1,0:T(8,128)S(1)}, u32[]{:S(2)}, u32[]{:S(2)}) collective-permute-start(f32[16,128]{1,0:T(8,128)S(1)} %get-tuple-element.133), channel_id=1, source_target_pairs={{1,0},{2,1},{3,2},{4,3},{5,4},{6,5},{7,6},{8,7},{9,8},{10,9},{11,1... | collective-permute-start | bytes 24584 | tf_op jit(solution)/shard_map/ppermute | solution.py:379
  115.2 2.9 %collective-permute-start.22 = (f32[48,128]{1,0:T(8,128)S(1)}, f32[48,128]{1,0:T(8,128)S(1)}, u32[]{:S(2)}, u32[]{:S(2)}) collective-permute-start(f32[48,128]{1,0:T(8,128)S(1)} %pad_maximum_fusion.17), channel_id=1, source_target_pairs={{32,0},{64,32},{96,64},{0,96},{33,1},{65,33},{97,65},{1,97},{34,2}... | collective-permute-start | bytes 73736 | tf_op jit(solution)/shard_map/ppermute | solution.py:382
  119.1 3.2 %collective-permute-done.23 = f32[48,128]{1,0:T(8,128)S(1)} collective-permute-done((f32[48,128]{1,0:T(8,128)S(1)}, f32[48,128]{1,0:T(8,128)S(1)}, u32[]{:S(2)}, u32[]{:S(2)}) %collective-permute-start.23) | collective-permute-done | bytes 24608 | tf_op jit(solution)/shard_map/ppermute | solution.py:382
  125.2 2.7 collective-permute-done.26
  127.9 9.3 %collective-permute-start.28 = (f32[256,128]{1,0:T(8,128)S(1)}, f32[256,128]{1,0:T(8,128)S(1)}, u32[]{:S(2)}, u32[]{:S(2)}) collective-permute-start(f32[256,128]{1,0:T(8,128)S(1)} %pad_maximum_fusion.9), channel_id=1, source_target_pairs={{2,0},{3,1},{4,2},{5,3},{6,4},{7,5},{0,6},{1,7},{10,8},{11,9},{12,... | collective-permute-start | bytes 393224 | tf_op jit(solution)/shard_map/ppermute | solution.py:379
  137.9 3.0 %collective-permute-done.28 = f32[256,128]{1,0:T(8,128)S(1)} collective-permute-done((f32[256,128]{1,0:T(8,128)S(1)}, f32[256,128]{1,0:T(8,128)S(1)}, u32[]{:S(2)}, u32[]{:S(2)}) %collective-permute-start.28) | collective-permute-done | bytes 131104 | tf_op jit(solution)/shard_map/ppermute | solution.py:379
  140.9 2.8 %collective-permute-done.29 = f32[256,128]{1,0:T(8,128)S(1)} collective-permute-done((f32[256,128]{1,0:T(8,128)S(1)}, f32[256,128]{1,0:T(8,128)S(1)}, u32[]{:S(2)}, u32[]{:S(2)}) %collective-permute-start.29) | collective-permute-done | bytes 131104 | tf_op jit(solution)/shard_map/ppermute | solution.py:379
  143.7 2.7 collective-permute-done.30
  147.5 2.7 collective-permute-start.35
  150.3 2.8 %collective-permute-done.33.refs_6_ = f32[4,128,128]{2,1,0:T(8,128)S(1)} collective-permute-done((f32[4,128,128]{2,1,0:T(8,128)S(1)}, f32[4,128,128]{2,1,0:T(8,128)S(1)}, u32[]{:S(2)}, u32[]{:S(2)}) %collective-permute-start.33) | collective-permute-done | bytes 262176 | tf_op jit(solution)/shard_map/ppermute | solution.py:379
  154.2 3.5 %update_1.1 = (f32[32,128,128]{2,1,0:T(8,128)S(1)}, bf16[32,128,128]{2,1,0:T(8,128)(2,1)S(1)}, f32[8,128]{1,0:T(8,128)S(1)}, f32[32,128,128]{2,1,0:T(8,128)S(1)}...) custom-call(s32[32]{0:T(128)S(1)} %bitcast.37, s32[128]{0:T(128)S(1)} %fusion.2.refs_1_, ...), custom_call_target="tpu_custom_call" | custom-call | tf_op jit(solution)/shard_map/update_1/pallas_call | solution.py:340
  157.8 8.7 %apply.4 = (f32[32,128,128]{2,1,0:T(8,128)S(1)}, f32[4,128,128]{2,1,0:T(8,128)S(1)}, f32[4,128,128]{2,1,0:T(8,128)S(1)}, f32[4,128,128]{2,1,0:T(8,128)S(1)}, f32...) custom-call(s32[32]{0:T(128)S(1)} %select_reduce_fusion.refs_0_, ...), custom_call_target="tpu_custom_call" | custom-call | tf_op jit(solution)/shard_map/apply/pallas_call | solution.py:200
  166.5 2.2 collective-permute-start.36
  168.6 3.5 %collective-permute-start.37 = (f32[16,128]{1,0:T(8,128)S(1)}, f32[16,128]{1,0:T(8,128)S(1)}, u32[]{:S(2)}, u32[]{:S(2)}) collective-permute-start(f32[16,128]{1,0:T(8,128)S(1)} %get-tuple-element.154), channel_id=1, source_target_pairs={{1,0},{2,1},{3,2},{4,3},{5,4},{6,5},{7,6},{8,7},{9,8},{10,9},{11,1... | collective-permute-start | bytes 24584 | tf_op jit(solution)/shard_map/ppermute | solution.py:379
  172.9 2.9 %collective-permute-start.38 = (f32[48,128]{1,0:T(8,128)S(1)}, f32[48,128]{1,0:T(8,128)S(1)}, u32[]{:S(2)}, u32[]{:S(2)}) collective-permute-start(f32[48,128]{1,0:T(8,128)S(1)} %pad_maximum_fusion.18), channel_id=1, source_target_pairs={{32,0},{64,32},{96,64},{0,96},{33,1},{65,33},{97,65},{1,97},{34,2}... | collective-permute-start | bytes 73736 | tf_op jit(solution)/shard_map/ppermute | solution.py:382
  176.8 3.2 %collective-permute-done.39 = f32[48,128]{1,0:T(8,128)S(1)} collective-permute-done((f32[48,128]{1,0:T(8,128)S(1)}, f32[48,128]{1,0:T(8,128)S(1)}, u32[]{:S(2)}, u32[]{:S(2)}) %collective-permute-start.39) | collective-permute-done | bytes 24608 | tf_op jit(solution)/shard_map/ppermute | solution.py:382
  181.6 1.3 collective-permute-done.41
  182.9 1.6 collective-permute-done.42
  185.3 9.7 %collective-permute-start.44 = (f32[256,128]{1,0:T(8,128)S(1)}, f32[256,128]{1,0:T(8,128)S(1)}, u32[]{:S(2)}, u32[]{:S(2)}) collective-permute-start(f32[256,128]{1,0:T(8,128)S(1)} %pad_maximum_fusion.10), channel_id=1, source_target_pairs={{2,0},{3,1},{4,2},{5,3},{6,4},{7,5},{0,6},{1,7},{10,8},{11,9},{12,... | collective-permute-start | bytes 393224 | tf_op jit(solution)/shard_map/ppermute | solution.py:379
  195.7 3.0 %collective-permute-done.44 = f32[256,128]{1,0:T(8,128)S(1)} collective-permute-done((f32[256,128]{1,0:T(8,128)S(1)}, f32[256,128]{1,0:T(8,128)S(1)}, u32[]{:S(2)}, u32[]{:S(2)}) %collective-permute-start.44) | collective-permute-done | bytes 131104 | tf_op jit(solution)/shard_map/ppermute | solution.py:379
  198.6 2.8 %collective-permute-done.45 = f32[256,128]{1,0:T(8,128)S(1)} collective-permute-done((f32[256,128]{1,0:T(8,128)S(1)}, f32[256,128]{1,0:T(8,128)S(1)}, u32[]{:S(2)}, u32[]{:S(2)}) %collective-permute-start.45) | collective-permute-done | bytes 131104 | tf_op jit(solution)/shard_map/ppermute | solution.py:379
  201.5 2.7 collective-permute-done.46
  205.2 2.7 collective-permute-start.51
  208.0 2.8 %collective-permute-done.49.refs_6_ = f32[4,128,128]{2,1,0:T(8,128)S(1)} collective-permute-done((f32[4,128,128]{2,1,0:T(8,128)S(1)}, f32[4,128,128]{2,1,0:T(8,128)S(1)}, u32[]{:S(2)}, u32[]{:S(2)}) %collective-permute-start.49) | collective-permute-done | bytes 262176 | tf_op jit(solution)/shard_map/ppermute | solution.py:379
  212.0 3.5 %update_2.1 = (f32[32,128,128]{2,1,0:T(8,128)S(1)}, bf16[32,128,128]{2,1,0:T(8,128)(2,1)S(1)}, f32[8,128]{1,0:T(8,128)S(1)}, f32[32,128,128]{2,1,0:T(8,128)S(1)}...) custom-call(s32[32]{0:T(128)S(1)} %bitcast.38, s32[128]{0:T(128)S(1)} %fusion.2.refs_1_, ...), custom_call_target="tpu_custom_call" | custom-call | tf_op jit(solution)/shard_map/update_2/pallas_call | solution.py:340
  215.5 1.3 copy-done.20
  216.8 9.5 %apply.5 = (f32[32,128,128]{2,1,0:T(8,128)S(1)}, f32[4,128,128]{2,1,0:T(8,128)}, f32[4,128,128]{2,1,0:T(8,128)}, f32[4,128,128]{2,1,0:T(8,128)S(1)}, f32[4,128,1...) custom-call(s32[32]{0:T(128)S(1)} %select_reduce_fusion.refs_0_, ...), custom_call_target="tpu_custom_call" | custom-call | tf_op jit(solution)/shard_map/apply/pallas_call | solution.py:200
  226.4 2.1 collective-permute-start.52
  228.4 3.4 %collective-permute-start.53 = (f32[16,128]{1,0:T(8,128)S(1)}, f32[16,128]{1,0:T(8,128)S(1)}, u32[]{:S(2)}, u32[]{:S(2)}) collective-permute-start(f32[16,128]{1,0:T(8,128)S(1)} %get-tuple-element.178), channel_id=1, source_target_pairs={{1,0},{2,1},{3,2},{4,3},{5,4},{6,5},{7,6},{8,7},{9,8},{10,9},{11,1... | collective-permute-start | bytes 24584 | tf_op jit(solution)/shard_map/ppermute | solution.py:379
  232.7 3.0 %collective-permute-start.54 = (f32[48,128]{1,0:T(8,128)S(1)}, f32[48,128]{1,0:T(8,128)S(1)}, u32[]{:S(2)}, u32[]{:S(2)}) collective-permute-start(f32[48,128]{1,0:T(8,128)S(1)} %pad_maximum_fusion.19), channel_id=1, source_target_pairs={{32,0},{64,32},{96,64},{0,96},{33,1},{65,33},{97,65},{1,97},{34,2}... | collective-permute-start | bytes 73736 | tf_op jit(solution)/shard_map/ppermute | solution.py:382
  236.6 3.2 %collective-permute-done.55 = f32[48,128]{1,0:T(8,128)S(1)} collective-permute-done((f32[48,128]{1,0:T(8,128)S(1)}, f32[48,128]{1,0:T(8,128)S(1)}, u32[]{:S(2)}, u32[]{:S(2)}) %collective-permute-start.55) | collective-permute-done | bytes 24608 | tf_op jit(solution)/shard_map/ppermute | solution.py:382
  242.7 1.6 collective-permute-done.58
  245.1 9.8 %collective-permute-start.60 = (f32[256,128]{1,0:T(8,128)S(1)}, f32[256,128]{1,0:T(8,128)S(1)}, u32[]{:S(2)}, u32[]{:S(2)}) collective-permute-start(f32[256,128]{1,0:T(8,128)S(1)} %pad_maximum_fusion.11), channel_id=1, source_target_pairs={{2,0},{3,1},{4,2},{5,3},{6,4},{7,5},{0,6},{1,7},{10,8},{11,9},{12,... | collective-permute-start | bytes 393224 | tf_op jit(solution)/shard_map/ppermute | solution.py:379
  255.6 3.0 %collective-permute-done.60 = f32[256,128]{1,0:T(8,128)S(1)} collective-permute-done((f32[256,128]{1,0:T(8,128)S(1)}, f32[256,128]{1,0:T(8,128)S(1)}, u32[]{:S(2)}, u32[]{:S(2)}) %collective-permute-start.60) | collective-permute-done | bytes 131104 | tf_op jit(solution)/shard_map/ppermute | solution.py:379
  258.5 2.8 %collective-permute-done.61 = f32[256,128]{1,0:T(8,128)S(1)} collective-permute-done((f32[256,128]{1,0:T(8,128)S(1)}, f32[256,128]{1,0:T(8,128)S(1)}, u32[]{:S(2)}, u32[]{:S(2)}) %collective-permute-start.61) | collective-permute-done | bytes 131104 | tf_op jit(solution)/shard_map/ppermute | solution.py:379
  261.3 2.7 collective-permute-done.62
  265.1 2.7 collective-permute-start.67
  267.8 2.5 multiply_add_fusion
  271.9 5.2 %update_3.1 = (f32[32,128,128]{2,1,0:T(8,128)}, f32[32,128,128]{2,1,0:T(8,128)}) custom-call(s32[32]{0:T(128)S(1)} %bitcast.39, s32[128]{0:T(128)S(1)} %fusion.2.refs_1_, f32[16]{0:T(128)S(1)} %pad_maximum_fusion.20.wm.refs_2_, f32[128,16,128]{2,1,0:T(8,128)S(1)} %bitcast.27, bf16[160,1536]{1,0:T(8,128)(2,1)S(1)} %copy-done.17, ...), custom_call_target="tpu_custom_call" | custom-call | tf_op jit(solution)/shard_map/update_3/pallas_call | solution.py:340
  (209 shorter events, 50.0 us)
Async XLA Ops:
  4.7 7.9 %collective-permute-start = (f32[16,2048]{1,0:T(8,128)S(1)}, f32[16,2048]{1,0:T(8,128)S(1)}, u32[]{:S(2)}, u32[]{:S(2)}) collective-permute-start(f32[16,2048]{1,0:T(8,128)S(1)} %get-tuple-element.102), channel_id=1, source_target_pairs={{31,0},{0,1},{1,2},{2,3},{3,4},{4,5},{5,6},{6,7},{7,8},{8,9},{9,10... | collective-permute-start | bytes 393224 | tf_op jit(solution)/shard_map/ppermute | solution.py:379
  7.3 5.3 %collective-permute-start.1 = (f32[16,2048]{1,0:T(8,128)S(1)}, f32[16,2048]{1,0:T(8,128)S(1)}, u32[]{:S(2)}, u32[]{:S(2)}) collective-permute-start(f32[16,2048]{1,0:T(8,128)S(1)} %get-tuple-element.103), channel_id=1, source_target_pairs={{1,0},{2,1},{3,2},{4,3},{5,4},{6,5},{7,6},{8,7},{9,8},{10,9},{11,1... | collective-permute-start | bytes 393224 | tf_op jit(solution)/shard_map/ppermute | solution.py:379
  7.3 6.1 %collective-permute-start.2 = (f32[16,2048]{1,0:T(8,128)S(1)}, f32[16,2048]{1,0:T(8,128)S(1)}, u32[]{:S(2)}, u32[]{:S(2)}) collective-permute-start(f32[16,2048]{1,0:T(8,128)S(1)} %get-tuple-element.104), channel_id=1, source_target_pairs={{96,0},{0,32},{32,64},{64,96},{97,1},{1,33},{33,65},{65,97},{98,2}... | collective-permute-start | bytes 393224 | tf_op jit(solution)/shard_map/ppermute | solution.py:382
  8.9 5.1 %collective-permute-start.3 = (f32[16,2048]{1,0:T(8,128)S(1)}, f32[16,2048]{1,0:T(8,128)S(1)}, u32[]{:S(2)}, u32[]{:S(2)}) collective-permute-start(f32[16,2048]{1,0:T(8,128)S(1)} %get-tuple-element.105), channel_id=1, source_target_pairs={{32,0},{64,32},{96,64},{0,96},{33,1},{65,33},{97,65},{1,97},{34,2}... | collective-permute-start | bytes 393224 | tf_op jit(solution)/shard_map/ppermute | solution.py:382
  44.4 5.5 %collective-permute-start.4 = (f32[16,128]{1,0:T(8,128)S(1)}, f32[16,128]{1,0:T(8,128)S(1)}, u32[]{:S(2)}, u32[]{:S(2)}) collective-permute-start(f32[16,128]{1,0:T(8,128)S(1)} %get-tuple-element.109), channel_id=1, source_target_pairs={{31,0},{0,1},{1,2},{2,3},{3,4},{4,5},{5,6},{6,7},{7,8},{8,9},{9,10... | collective-permute-start | bytes 24584 | tf_op jit(solution)/shard_map/ppermute | solution.py:379
  47.5 3.1 %collective-permute-start.5 = (f32[16,128]{1,0:T(8,128)S(1)}, f32[16,128]{1,0:T(8,128)S(1)}, u32[]{:S(2)}, u32[]{:S(2)}) collective-permute-start(f32[16,128]{1,0:T(8,128)S(1)} %get-tuple-element.110), channel_id=1, source_target_pairs={{1,0},{2,1},{3,2},{4,3},{5,4},{6,5},{7,6},{8,7},{9,8},{10,9},{11,1... | collective-permute-start | bytes 24584 | tf_op jit(solution)/shard_map/ppermute | solution.py:379
  52.7 4.3 %collective-permute-start.7 = (f32[48,128]{1,0:T(8,128)S(1)}, f32[48,128]{1,0:T(8,128)S(1)}, u32[]{:S(2)}, u32[]{:S(2)}) collective-permute-start(f32[48,128]{1,0:T(8,128)S(1)} %pad_maximum_fusion.16), channel_id=1, source_target_pairs={{64,0},{96,32},{0,64},{32,96},{65,1},{97,33},{1,65},{33,97},{66,2}... | collective-permute-start | bytes 73736 | tf_op jit(solution)/shard_map/ppermute | solution.py:382
  52.9 4.2 %collective-permute-start.8 = (f32[48,128]{1,0:T(8,128)S(1)}, f32[48,128]{1,0:T(8,128)S(1)}, u32[]{:S(2)}, u32[]{:S(2)}) collective-permute-start(f32[48,128]{1,0:T(8,128)S(1)} %pad_maximum_fusion.16), channel_id=1, source_target_pairs={{96,0},{0,32},{32,64},{64,96},{97,1},{1,33},{33,65},{65,97},{98,2}... | collective-permute-start | bytes 73736 | tf_op jit(solution)/shard_map/ppermute | solution.py:382
  57.0 5.6 %collective-permute-start.10 = (f32[64,128]{1,0:T(8,128)S(1)}, f32[64,128]{1,0:T(8,128)S(1)}, u32[]{:S(2)}, u32[]{:S(2)}) collective-permute-start(f32[64,128]{1,0:T(8,128)S(1)} %pad_maximum_fusion.12), channel_id=1, source_target_pairs={{16,0},{17,1},{18,2},{19,3},{20,4},{21,5},{22,6},{23,7},{24,8},{25... | collective-permute-start | bytes 98312 | tf_op jit(solution)/shard_map/ppermute | solution.py:379
  60.0 4.0 %collective-permute-start.11 = (f32[64,128]{1,0:T(8,128)S(1)}, f32[64,128]{1,0:T(8,128)S(1)}, u32[]{:S(2)}, u32[]{:S(2)}) collective-permute-start(f32[64,128]{1,0:T(8,128)S(1)} %pad_maximum_fusion.12), channel_id=1, source_target_pairs={{24,0},{25,1},{26,2},{27,3},{28,4},{29,5},{30,6},{31,7},{0,8},{1,9... | collective-permute-start | bytes 98312 | tf_op jit(solution)/shard_map/ppermute | solution.py:379
  60.4 3.6 %collective-permute-start.9 = (f32[64,128]{1,0:T(8,128)S(1)}, f32[64,128]{1,0:T(8,128)S(1)}, u32[]{:S(2)}, u32[]{:S(2)}) collective-permute-start(f32[64,128]{1,0:T(8,128)S(1)} %pad_maximum_fusion.12), channel_id=1, source_target_pairs={{8,0},{9,1},{10,2},{11,3},{12,4},{13,5},{14,6},{15,7},{16,8},{17,9... | collective-permute-start | bytes 98312 | tf_op jit(solution)/shard_map/ppermute | solution.py:379
  64.0 12.4 %collective-permute-start.12 = (f32[256,128]{1,0:T(8,128)S(1)}, f32[256,128]{1,0:T(8,128)S(1)}, u32[]{:S(2)}, u32[]{:S(2)}) collective-permute-start(f32[256,128]{1,0:T(8,128)S(1)} %pad_maximum_fusion.8), channel_id=1, source_target_pairs={{2,0},{3,1},{4,2},{5,3},{6,4},{7,5},{0,6},{1,7},{10,8},{11,9},{12,... | collective-permute-start | bytes 393224 | tf_op jit(solution)/shard_map/ppermute | solution.py:379
  70.9 6.8 %collective-permute-start.13 = (f32[256,128]{1,0:T(8,128)S(1)}, f32[256,128]{1,0:T(8,128)S(1)}, u32[]{:S(2)}, u32[]{:S(2)}) collective-permute-start(f32[256,128]{1,0:T(8,128)S(1)} %pad_maximum_fusion.8), channel_id=1, source_target_pairs={{4,0},{5,1},{6,2},{7,3},{0,4},{1,5},{2,6},{3,7},{12,8},{13,9},{14,... | collective-permute-start | bytes 393224 | tf_op jit(solution)/shard_map/ppermute | solution.py:379
  70.9 9.4 %collective-permute-start.14 = (f32[256,128]{1,0:T(8,128)S(1)}, f32[256,128]{1,0:T(8,128)S(1)}, u32[]{:S(2)}, u32[]{:S(2)}) collective-permute-start(f32[256,128]{1,0:T(8,128)S(1)} %pad_maximum_fusion.8), channel_id=1, source_target_pairs={{6,0},{7,1},{0,2},{1,3},{2,4},{3,5},{4,6},{5,7},{14,8},{15,9},{8,1... | collective-permute-start | bytes 393224 | tf_op jit(solution)/shard_map/ppermute | solution.py:379
  81.1 3.7 %collective-permute-start.15 = (f32[1024,128]{1,0:T(8,128)}, f32[1024,128]{1,0:T(8,128)}, u32[]{:S(2)}, u32[]{:S(2)}) collective-permute-start(f32[1024,128]{1,0:T(8,128)} %pad_maximum_fusion.4), channel_id=1, source_target_pairs={{1,0},{0,1},{3,2},{2,3},{5,4},{4,5},{7,6},{6,7},{9,8},{8,9},{11,10... | collective-permute-start | bytes 1572872 | tf_op jit(solution)/shard_map/ppermute | solution.py:379
  81.7 4.5 %collective-permute-start.16 = (f32[4,128,128]{2,1,0:T(8,128)}, f32[4,128,128]{2,1,0:T(8,128)S(1)}, u32[]{:S(2)}, u32[]{:S(2)}) collective-permute-start(f32[4,128,128]{2,1,0:T(8,128)} %copy-done.39), channel_id=1, source_target_pairs={{31,0},{0,1},{1,2},{2,3},{3,4},{4,5},{5,6},{6,7},{7,8},{8,9},{9,10... | collective-permute-start | bytes 786440 | tf_op jit(solution)/shard_map/ppermute | solution.py:379
  81.7 6.3 %collective-permute-start.17 = (f32[4,128,128]{2,1,0:T(8,128)}, f32[4,128,128]{2,1,0:T(8,128)S(1)}, u32[]{:S(2)}, u32[]{:S(2)}) collective-permute-start(f32[4,128,128]{2,1,0:T(8,128)} %copy-done.38), channel_id=1, source_target_pairs={{1,0},{2,1},{3,2},{4,3},{5,4},{6,5},{7,6},{8,7},{9,8},{10,9},{11,1... | collective-permute-start | bytes 786440 | tf_op jit(solution)/shard_map/ppermute | solution.py:379
  82.2 6.9 %collective-permute-start.18 = (f32[4,128,128]{2,1,0:T(8,128)}, f32[4,128,128]{2,1,0:T(8,128)S(1)}, u32[]{:S(2)}, u32[]{:S(2)}) collective-permute-start(f32[4,128,128]{2,1,0:T(8,128)} %copy-done.37), channel_id=1, source_target_pairs={{96,0},{0,32},{32,64},{64,96},{97,1},{1,33},{33,65},{65,97},{98,2}... | collective-permute-start | bytes 786440 | tf_op jit(solution)/shard_map/ppermute | solution.py:382
  82.2 6.9 %collective-permute-start.19 = (f32[4,128,128]{2,1,0:T(8,128)}, f32[4,128,128]{2,1,0:T(8,128)S(1)}, u32[]{:S(2)}, u32[]{:S(2)}) collective-permute-start(f32[4,128,128]{2,1,0:T(8,128)} %copy-done.36), channel_id=1, source_target_pairs={{32,0},{64,32},{96,64},{0,96},{33,1},{65,33},{97,65},{1,97},{34,2}... | collective-permute-start | bytes 786440 | tf_op jit(solution)/shard_map/ppermute | solution.py:382
  108.6 6.3 %collective-permute-start.20 = (f32[16,128]{1,0:T(8,128)S(1)}, f32[16,128]{1,0:T(8,128)S(1)}, u32[]{:S(2)}, u32[]{:S(2)}) collective-permute-start(f32[16,128]{1,0:T(8,128)S(1)} %get-tuple-element.132), channel_id=1, source_target_pairs={{31,0},{0,1},{1,2},{2,3},{3,4},{4,5},{5,6},{6,7},{7,8},{8,9},{9,10... | collective-permute-start | bytes 24584 | tf_op jit(solution)/shard_map/ppermute | solution.py:379
  110.9 4.2 %collective-permute-start.21 = (f32[16,128]{1,0:T(8,128)S(1)}, f32[16,128]{1,0:T(8,128)S(1)}, u32[]{:S(2)}, u32[]{:S(2)}) collective-permute-start(f32[16,128]{1,0:T(8,128)S(1)} %get-tuple-element.133), channel_id=1, source_target_pairs={{1,0},{2,1},{3,2},{4,3},{5,4},{6,5},{7,6},{8,7},{9,8},{10,9},{11,1... | collective-permute-start | bytes 24584 | tf_op jit(solution)/shard_map/ppermute | solution.py:379
  115.2 3.9 %collective-permute-start.22 = (f32[48,128]{1,0:T(8,128)S(1)}, f32[48,128]{1,0:T(8,128)S(1)}, u32[]{:S(2)}, u32[]{:S(2)}) collective-permute-start(f32[48,128]{1,0:T(8,128)S(1)} %pad_maximum_fusion.17), channel_id=1, source_target_pairs={{32,0},{64,32},{96,64},{0,96},{33,1},{65,33},{97,65},{1,97},{34,2}... | collective-permute-start | bytes 73736 | tf_op jit(solution)/shard_map/ppermute | solution.py:382
  118.1 4.2 %collective-permute-start.23 = (f32[48,128]{1,0:T(8,128)S(1)}, f32[48,128]{1,0:T(8,128)S(1)}, u32[]{:S(2)}, u32[]{:S(2)}) collective-permute-start(f32[48,128]{1,0:T(8,128)S(1)} %pad_maximum_fusion.17), channel_id=1, source_target_pairs={{64,0},{96,32},{0,64},{32,96},{65,1},{97,33},{1,65},{33,97},{66,2}... | collective-permute-start | bytes 73736 | tf_op jit(solution)/shard_map/ppermute | solution.py:382
  118.1 4.2 %collective-permute-start.24 = (f32[48,128]{1,0:T(8,128)S(1)}, f32[48,128]{1,0:T(8,128)S(1)}, u32[]{:S(2)}, u32[]{:S(2)}) collective-permute-start(f32[48,128]{1,0:T(8,128)S(1)} %pad_maximum_fusion.17), channel_id=1, source_target_pairs={{96,0},{0,32},{32,64},{64,96},{97,1},{1,33},{33,65},{65,97},{98,2}... | collective-permute-start | bytes 73736 | tf_op jit(solution)/shard_map/ppermute | solution.py:382
  123.5 4.4 %collective-permute-start.26 = (f32[64,128]{1,0:T(8,128)S(1)}, f32[64,128]{1,0:T(8,128)S(1)}, u32[]{:S(2)}, u32[]{:S(2)}) collective-permute-start(f32[64,128]{1,0:T(8,128)S(1)} %pad_maximum_fusion.13), channel_id=1, source_target_pairs={{16,0},{17,1},{18,2},{19,3},{20,4},{21,5},{22,6},{23,7},{24,8},{25... | collective-permute-start | bytes 98312 | tf_op jit(solution)/shard_map/ppermute | solution.py:379
  123.5 4.4 %collective-permute-start.27 = (f32[64,128]{1,0:T(8,128)S(1)}, f32[64,128]{1,0:T(8,128)S(1)}, u32[]{:S(2)}, u32[]{:S(2)}) collective-permute-start(f32[64,128]{1,0:T(8,128)S(1)} %pad_maximum_fusion.13), channel_id=1, source_target_pairs={{24,0},{25,1},{26,2},{27,3},{28,4},{29,5},{30,6},{31,7},{0,8},{1,9... | collective-permute-start | bytes 98312 | tf_op jit(solution)/shard_map/ppermute | solution.py:379
  127.9 13.0 %collective-permute-start.28 = (f32[256,128]{1,0:T(8,128)S(1)}, f32[256,128]{1,0:T(8,128)S(1)}, u32[]{:S(2)}, u32[]{:S(2)}) collective-permute-start(f32[256,128]{1,0:T(8,128)S(1)} %pad_maximum_fusion.9), channel_id=1, source_target_pairs={{2,0},{3,1},{4,2},{5,3},{6,4},{7,5},{0,6},{1,7},{10,8},{11,9},{12,... | collective-permute-start | bytes 393224 | tf_op jit(solution)/shard_map/ppermute | solution.py:379
  137.2 6.4 %collective-permute-start.29 = (f32[256,128]{1,0:T(8,128)S(1)}, f32[256,128]{1,0:T(8,128)S(1)}, u32[]{:S(2)}, u32[]{:S(2)}) collective-permute-start(f32[256,128]{1,0:T(8,128)S(1)} %pad_maximum_fusion.9), channel_id=1, source_target_pairs={{4,0},{5,1},{6,2},{7,3},{0,4},{1,5},{2,6},{3,7},{12,8},{13,9},{14,... | collective-permute-start | bytes 393224 | tf_op jit(solution)/shard_map/ppermute | solution.py:379
  137.3 9.1 %collective-permute-start.30 = (f32[256,128]{1,0:T(8,128)S(1)}, f32[256,128]{1,0:T(8,128)S(1)}, u32[]{:S(2)}, u32[]{:S(2)}) collective-permute-start(f32[256,128]{1,0:T(8,128)S(1)} %pad_maximum_fusion.9), channel_id=1, source_target_pairs={{6,0},{7,1},{0,2},{1,3},{2,4},{3,5},{4,6},{5,7},{14,8},{15,9},{8,1... | collective-permute-start | bytes 393224 | tf_op jit(solution)/shard_map/ppermute | solution.py:379
  146.4 3.7 %collective-permute-start.31 = (f32[1024,128]{1,0:T(8,128)S(1)}, f32[1024,128]{1,0:T(8,128)S(1)}, u32[]{:S(2)}, u32[]{:S(2)}) collective-permute-start(f32[1024,128]{1,0:T(8,128)S(1)} %pad_maximum_fusion.5), channel_id=1, source_target_pairs={{1,0},{0,1},{3,2},{2,3},{5,4},{4,5},{7,6},{6,7},{9,8},{8,9},{11,10... | collective-permute-start | bytes 1572872 | tf_op jit(solution)/shard_map/ppermute | solution.py:379
  146.9 3.3 %collective-permute-start.32 = (f32[4,128,128]{2,1,0:T(8,128)S(1)}, f32[4,128,128]{2,1,0:T(8,128)S(1)}, u32[]{:S(2)}, u32[]{:S(2)}) collective-permute-start(f32[4,128,128]{2,1,0:T(8,128)S(1)} %get-tuple-element.144), channel_id=1, source_target_pairs={{31,0},{0,1},{1,2},{2,3},{3,4},{4,5},{5,6},{6,7},{7,8},{8,9},{9,10... | collective-permute-start | bytes 786440 | tf_op jit(solution)/shard_map/ppermute | solution.py:379
  147.0 6.1 %collective-permute-start.33 = (f32[4,128,128]{2,1,0:T(8,128)S(1)}, f32[4,128,128]{2,1,0:T(8,128)S(1)}, u32[]{:S(2)}, u32[]{:S(2)}) collective-permute-start(f32[4,128,128]{2,1,0:T(8,128)S(1)} %get-tuple-element.145), channel_id=1, source_target_pairs={{1,0},{2,1},{3,2},{4,3},{5,4},{6,5},{7,6},{8,7},{9,8},{10,9},{11,1... | collective-permute-start | bytes 786440 | tf_op jit(solution)/shard_map/ppermute | solution.py:379
  147.5 6.7 %collective-permute-start.34 = (f32[4,128,128]{2,1,0:T(8,128)S(1)}, f32[4,128,128]{2,1,0:T(8,128)S(1)}, u32[]{:S(2)}, u32[]{:S(2)}) collective-permute-start(f32[4,128,128]{2,1,0:T(8,128)S(1)} %get-tuple-element.146), channel_id=1, source_target_pairs={{96,0},{0,32},{32,64},{64,96},{97,1},{1,33},{33,65},{65,97},{98,2}... | collective-permute-start | bytes 786440 | tf_op jit(solution)/shard_map/ppermute | solution.py:382
  147.5 6.7 %collective-permute-start.35 = (f32[4,128,128]{2,1,0:T(8,128)S(1)}, f32[4,128,128]{2,1,0:T(8,128)S(1)}, u32[]{:S(2)}, u32[]{:S(2)}) collective-permute-start(f32[4,128,128]{2,1,0:T(8,128)S(1)} %get-tuple-element.147), channel_id=1, source_target_pairs={{32,0},{64,32},{96,64},{0,96},{33,1},{65,33},{97,65},{1,97},{34,2}... | collective-permute-start | bytes 786440 | tf_op jit(solution)/shard_map/ppermute | solution.py:382
  166.5 6.2 %collective-permute-start.36 = (f32[16,128]{1,0:T(8,128)S(1)}, f32[16,128]{1,0:T(8,128)S(1)}, u32[]{:S(2)}, u32[]{:S(2)}) collective-permute-start(f32[16,128]{1,0:T(8,128)S(1)} %get-tuple-element.153), channel_id=1, source_target_pairs={{31,0},{0,1},{1,2},{2,3},{3,4},{4,5},{5,6},{6,7},{7,8},{8,9},{9,10... | collective-permute-start | bytes 24584 | tf_op jit(solution)/shard_map/ppermute | solution.py:379
  168.6 4.3 %collective-permute-start.37 = (f32[16,128]{1,0:T(8,128)S(1)}, f32[16,128]{1,0:T(8,128)S(1)}, u32[]{:S(2)}, u32[]{:S(2)}) collective-permute-start(f32[16,128]{1,0:T(8,128)S(1)} %get-tuple-element.154), channel_id=1, source_target_pairs={{1,0},{2,1},{3,2},{4,3},{5,4},{6,5},{7,6},{8,7},{9,8},{10,9},{11,1... | collective-permute-start | bytes 24584 | tf_op jit(solution)/shard_map/ppermute | solution.py:379
  172.9 3.9 %collective-permute-start.38 = (f32[48,128]{1,0:T(8,128)S(1)}, f32[48,128]{1,0:T(8,128)S(1)}, u32[]{:S(2)}, u32[]{:S(2)}) collective-permute-start(f32[48,128]{1,0:T(8,128)S(1)} %pad_maximum_fusion.18), channel_id=1, source_target_pairs={{32,0},{64,32},{96,64},{0,96},{33,1},{65,33},{97,65},{1,97},{34,2}... | collective-permute-start | bytes 73736 | tf_op jit(solution)/shard_map/ppermute | solution.py:382
  175.9 4.2 %collective-permute-start.39 = (f32[48,128]{1,0:T(8,128)S(1)}, f32[48,128]{1,0:T(8,128)S(1)}, u32[]{:S(2)}, u32[]{:S(2)}) collective-permute-start(f32[48,128]{1,0:T(8,128)S(1)} %pad_maximum_fusion.18), channel_id=1, source_target_pairs={{64,0},{96,32},{0,64},{32,96},{65,1},{97,33},{1,65},{33,97},{66,2}... | collective-permute-start | bytes 73736 | tf_op jit(solution)/shard_map/ppermute | solution.py:382
  175.9 4.2 %collective-permute-start.40 = (f32[48,128]{1,0:T(8,128)S(1)}, f32[48,128]{1,0:T(8,128)S(1)}, u32[]{:S(2)}, u32[]{:S(2)}) collective-permute-start(f32[48,128]{1,0:T(8,128)S(1)} %pad_maximum_fusion.18), channel_id=1, source_target_pairs={{96,0},{0,32},{32,64},{64,96},{97,1},{1,33},{33,65},{65,97},{98,2}... | collective-permute-start | bytes 73736 | tf_op jit(solution)/shard_map/ppermute | solution.py:382
  180.2 4.3 %collective-permute-start.42 = (f32[64,128]{1,0:T(8,128)S(1)}, f32[64,128]{1,0:T(8,128)S(1)}, u32[]{:S(2)}, u32[]{:S(2)}) collective-permute-start(f32[64,128]{1,0:T(8,128)S(1)} %pad_maximum_fusion.14), channel_id=1, source_target_pairs={{16,0},{17,1},{18,2},{19,3},{20,4},{21,5},{22,6},{23,7},{24,8},{25... | collective-permute-start | bytes 98312 | tf_op jit(solution)/shard_map/ppermute | solution.py:379
  180.6 4.8 %collective-permute-start.43 = (f32[64,128]{1,0:T(8,128)S(1)}, f32[64,128]{1,0:T(8,128)S(1)}, u32[]{:S(2)}, u32[]{:S(2)}) collective-permute-start(f32[64,128]{1,0:T(8,128)S(1)} %pad_maximum_fusion.14), channel_id=1, source_target_pairs={{24,0},{25,1},{26,2},{27,3},{28,4},{29,5},{30,6},{31,7},{0,8},{1,9... | collective-permute-start | bytes 98312 | tf_op jit(solution)/shard_map/ppermute | solution.py:379
  185.3 13.3 %collective-permute-start.44 = (f32[256,128]{1,0:T(8,128)S(1)}, f32[256,128]{1,0:T(8,128)S(1)}, u32[]{:S(2)}, u32[]{:S(2)}) collective-permute-start(f32[256,128]{1,0:T(8,128)S(1)} %pad_maximum_fusion.10), channel_id=1, source_target_pairs={{2,0},{3,1},{4,2},{5,3},{6,4},{7,5},{0,6},{1,7},{10,8},{11,9},{12,... | collective-permute-start | bytes 393224 | tf_op jit(solution)/shard_map/ppermute | solution.py:379
  195.0 6.4 %collective-permute-start.45 = (f32[256,128]{1,0:T(8,128)S(1)}, f32[256,128]{1,0:T(8,128)S(1)}, u32[]{:S(2)}, u32[]{:S(2)}) collective-permute-start(f32[256,128]{1,0:T(8,128)S(1)} %pad_maximum_fusion.10), channel_id=1, source_target_pairs={{4,0},{5,1},{6,2},{7,3},{0,4},{1,5},{2,6},{3,7},{12,8},{13,9},{14,... | collective-permute-start | bytes 393224 | tf_op jit(solution)/shard_map/ppermute | solution.py:379
  195.0 9.1 %collective-permute-start.46 = (f32[256,128]{1,0:T(8,128)S(1)}, f32[256,128]{1,0:T(8,128)S(1)}, u32[]{:S(2)}, u32[]{:S(2)}) collective-permute-start(f32[256,128]{1,0:T(8,128)S(1)} %pad_maximum_fusion.10), channel_id=1, source_target_pairs={{6,0},{7,1},{0,2},{1,3},{2,4},{3,5},{4,6},{5,7},{14,8},{15,9},{8,1... | collective-permute-start | bytes 393224 | tf_op jit(solution)/shard_map/ppermute | solution.py:379
  204.2 3.7 %collective-permute-start.47 = (f32[1024,128]{1,0:T(8,128)S(1)}, f32[1024,128]{1,0:T(8,128)S(1)}, u32[]{:S(2)}, u32[]{:S(2)}) collective-permute-start(f32[1024,128]{1,0:T(8,128)S(1)} %pad_maximum_fusion.6), channel_id=1, source_target_pairs={{1,0},{0,1},{3,2},{2,3},{5,4},{4,5},{7,6},{6,7},{9,8},{8,9},{11,10... | collective-permute-start | bytes 1572872 | tf_op jit(solution)/shard_map/ppermute | solution.py:379
  204.7 3.3 %collective-permute-start.48 = (f32[4,128,128]{2,1,0:T(8,128)S(1)}, f32[4,128,128]{2,1,0:T(8,128)S(1)}, u32[]{:S(2)}, u32[]{:S(2)}) collective-permute-start(f32[4,128,128]{2,1,0:T(8,128)S(1)} %get-tuple-element.165), channel_id=1, source_target_pairs={{31,0},{0,1},{1,2},{2,3},{3,4},{4,5},{5,6},{6,7},{7,8},{8,9},{9,10... | collective-permute-start | bytes 786440 | tf_op jit(solution)/shard_map/ppermute | solution.py:379
  204.7 6.1 %collective-permute-start.49 = (f32[4,128,128]{2,1,0:T(8,128)S(1)}, f32[4,128,128]{2,1,0:T(8,128)S(1)}, u32[]{:S(2)}, u32[]{:S(2)}) collective-permute-start(f32[4,128,128]{2,1,0:T(8,128)S(1)} %get-tuple-element.166), channel_id=1, source_target_pairs={{1,0},{2,1},{3,2},{4,3},{5,4},{6,5},{7,6},{8,7},{9,8},{10,9},{11,1... | collective-permute-start | bytes 786440 | tf_op jit(solution)/shard_map/ppermute | solution.py:379
  205.2 6.7 %collective-permute-start.50 = (f32[4,128,128]{2,1,0:T(8,128)S(1)}, f32[4,128,128]{2,1,0:T(8,128)S(1)}, u32[]{:S(2)}, u32[]{:S(2)}) collective-permute-start(f32[4,128,128]{2,1,0:T(8,128)S(1)} %get-tuple-element.167), channel_id=1, source_target_pairs={{96,0},{0,32},{32,64},{64,96},{97,1},{1,33},{33,65},{65,97},{98,2}... | collective-permute-start | bytes 786440 | tf_op jit(solution)/shard_map/ppermute | solution.py:382
  205.2 6.7 %collective-permute-start.51 = (f32[4,128,128]{2,1,0:T(8,128)S(1)}, f32[4,128,128]{2,1,0:T(8,128)S(1)}, u32[]{:S(2)}, u32[]{:S(2)}) collective-permute-start(f32[4,128,128]{2,1,0:T(8,128)S(1)} %get-tuple-element.168), channel_id=1, source_target_pairs={{32,0},{64,32},{96,64},{0,96},{33,1},{65,33},{97,65},{1,97},{34,2}... | collective-permute-start | bytes 786440 | tf_op jit(solution)/shard_map/ppermute | solution.py:382
  226.4 6.2 %collective-permute-start.52 = (f32[16,128]{1,0:T(8,128)S(1)}, f32[16,128]{1,0:T(8,128)S(1)}, u32[]{:S(2)}, u32[]{:S(2)}) collective-permute-start(f32[16,128]{1,0:T(8,128)S(1)} %get-tuple-element.177), channel_id=1, source_target_pairs={{31,0},{0,1},{1,2},{2,3},{3,4},{4,5},{5,6},{6,7},{7,8},{8,9},{9,10... | collective-permute-start | bytes 24584 | tf_op jit(solution)/shard_map/ppermute | solution.py:379
  228.4 4.3 %collective-permute-start.53 = (f32[16,128]{1,0:T(8,128)S(1)}, f32[16,128]{1,0:T(8,128)S(1)}, u32[]{:S(2)}, u32[]{:S(2)}) collective-permute-start(f32[16,128]{1,0:T(8,128)S(1)} %get-tuple-element.178), channel_id=1, source_target_pairs={{1,0},{2,1},{3,2},{4,3},{5,4},{6,5},{7,6},{8,7},{9,8},{10,9},{11,1... | collective-permute-start | bytes 24584 | tf_op jit(solution)/shard_map/ppermute | solution.py:379
  232.7 3.9 %collective-permute-start.54 = (f32[48,128]{1,0:T(8,128)S(1)}, f32[48,128]{1,0:T(8,128)S(1)}, u32[]{:S(2)}, u32[]{:S(2)}) collective-permute-start(f32[48,128]{1,0:T(8,128)S(1)} %pad_maximum_fusion.19), channel_id=1, source_target_pairs={{32,0},{64,32},{96,64},{0,96},{33,1},{65,33},{97,65},{1,97},{34,2}... | collective-permute-start | bytes 73736 | tf_op jit(solution)/shard_map/ppermute | solution.py:382
  235.7 4.2 %collective-permute-start.55 = (f32[48,128]{1,0:T(8,128)S(1)}, f32[48,128]{1,0:T(8,128)S(1)}, u32[]{:S(2)}, u32[]{:S(2)}) collective-permute-start(f32[48,128]{1,0:T(8,128)S(1)} %pad_maximum_fusion.19), channel_id=1, source_target_pairs={{64,0},{96,32},{0,64},{32,96},{65,1},{97,33},{1,65},{33,97},{66,2}... | collective-permute-start | bytes 73736 | tf_op jit(solution)/shard_map/ppermute | solution.py:382
  235.7 4.2 %collective-permute-start.56 = (f32[48,128]{1,0:T(8,128)S(1)}, f32[48,128]{1,0:T(8,128)S(1)}, u32[]{:S(2)}, u32[]{:S(2)}) collective-permute-start(f32[48,128]{1,0:T(8,128)S(1)} %pad_maximum_fusion.19), channel_id=1, source_target_pairs={{96,0},{0,32},{32,64},{64,96},{97,1},{1,33},{33,65},{65,97},{98,2}... | collective-permute-start | bytes 73736 | tf_op jit(solution)/shard_map/ppermute | solution.py:382
  240.0 4.3 %collective-permute-start.58 = (f32[64,128]{1,0:T(8,128)S(1)}, f32[64,128]{1,0:T(8,128)S(1)}, u32[]{:S(2)}, u32[]{:S(2)}) collective-permute-start(f32[64,128]{1,0:T(8,128)S(1)} %pad_maximum_fusion.15), channel_id=1, source_target_pairs={{16,0},{17,1},{18,2},{19,3},{20,4},{21,5},{22,6},{23,7},{24,8},{25... | collective-permute-start | bytes 98312 | tf_op jit(solution)/shard_map/ppermute | solution.py:379
  240.4 4.7 %collective-permute-start.59 = (f32[64,128]{1,0:T(8,128)S(1)}, f32[64,128]{1,0:T(8,128)S(1)}, u32[]{:S(2)}, u32[]{:S(2)}) collective-permute-start(f32[64,128]{1,0:T(8,128)S(1)} %pad_maximum_fusion.15), channel_id=1, source_target_pairs={{24,0},{25,1},{26,2},{27,3},{28,4},{29,5},{30,6},{31,7},{0,8},{1,9... | collective-permute-start | bytes 98312 | tf_op jit(solution)/shard_map/ppermute | solution.py:379
  245.1 13.4 %collective-permute-start.60 = (f32[256,128]{1,0:T(8,128)S(1)}, f32[256,128]{1,0:T(8,128)S(1)}, u32[]{:S(2)}, u32[]{:S(2)}) collective-permute-start(f32[256,128]{1,0:T(8,128)S(1)} %pad_maximum_fusion.11), channel_id=1, source_target_pairs={{2,0},{3,1},{4,2},{5,3},{6,4},{7,5},{0,6},{1,7},{10,8},{11,9},{12,... | collective-permute-start | bytes 393224 | tf_op jit(solution)/shard_map/ppermute | solution.py:379
  254.9 6.4 %collective-permute-start.61 = (f32[256,128]{1,0:T(8,128)S(1)}, f32[256,128]{1,0:T(8,128)S(1)}, u32[]{:S(2)}, u32[]{:S(2)}) collective-permute-start(f32[256,128]{1,0:T(8,128)S(1)} %pad_maximum_fusion.11), channel_id=1, source_target_pairs={{4,0},{5,1},{6,2},{7,3},{0,4},{1,5},{2,6},{3,7},{12,8},{13,9},{14,... | collective-permute-start | bytes 393224 | tf_op jit(solution)/shard_map/ppermute | solution.py:379
  254.9 9.1 %collective-permute-start.62 = (f32[256,128]{1,0:T(8,128)S(1)}, f32[256,128]{1,0:T(8,128)S(1)}, u32[]{:S(2)}, u32[]{:S(2)}) collective-permute-start(f32[256,128]{1,0:T(8,128)S(1)} %pad_maximum_fusion.11), channel_id=1, source_target_pairs={{6,0},{7,1},{0,2},{1,3},{2,4},{3,5},{4,6},{5,7},{14,8},{15,9},{8,1... | collective-permute-start | bytes 393224 | tf_op jit(solution)/shard_map/ppermute | solution.py:379
  264.0 6.2 %collective-permute-start.63 = (f32[1024,128]{1,0:T(8,128)S(1)}, f32[1024,128]{1,0:T(8,128)S(1)}, u32[]{:S(2)}, u32[]{:S(2)}) collective-permute-start(f32[1024,128]{1,0:T(8,128)S(1)} %pad_maximum_fusion.7), channel_id=1, source_target_pairs={{1,0},{0,1},{3,2},{2,3},{5,4},{4,5},{7,6},{6,7},{9,8},{8,9},{11,10... | collective-permute-start | bytes 1572872 | tf_op jit(solution)/shard_map/ppermute | solution.py:379
  264.6 5.8 %collective-permute-start.64 = (f32[4,128,128]{2,1,0:T(8,128)}, f32[4,128,128]{2,1,0:T(8,128)S(1)}, u32[]{:S(2)}, u32[]{:S(2)}) collective-permute-start(f32[4,128,128]{2,1,0:T(8,128)} %get-tuple-element.189), channel_id=1, source_target_pairs={{31,0},{0,1},{1,2},{2,3},{3,4},{4,5},{5,6},{6,7},{7,8},{8,9},{9,10... | collective-permute-start | bytes 786440 | tf_op jit(solution)/shard_map/ppermute | solution.py:379
  264.6 6.3 %collective-permute-start.65 = (f32[4,128,128]{2,1,0:T(8,128)}, f32[4,128,128]{2,1,0:T(8,128)S(1)}, u32[]{:S(2)}, u32[]{:S(2)}) collective-permute-start(f32[4,128,128]{2,1,0:T(8,128)} %get-tuple-element.190), channel_id=1, source_target_pairs={{1,0},{2,1},{3,2},{4,3},{5,4},{6,5},{7,6},{8,7},{9,8},{10,9},{11,1... | collective-permute-start | bytes 786440 | tf_op jit(solution)/shard_map/ppermute | solution.py:379
  265.1 6.7 %collective-permute-start.66 = (f32[4,128,128]{2,1,0:T(8,128)S(1)}, f32[4,128,128]{2,1,0:T(8,128)S(1)}, u32[]{:S(2)}, u32[]{:S(2)}) collective-permute-start(f32[4,128,128]{2,1,0:T(8,128)S(1)} %get-tuple-element.191), channel_id=1, source_target_pairs={{96,0},{0,32},{32,64},{64,96},{97,1},{1,33},{33,65},{65,97},{98,2}... | collective-permute-start | bytes 786440 | tf_op jit(solution)/shard_map/ppermute | solution.py:382
  265.1 6.7 %collective-permute-start.67 = (f32[4,128,128]{2,1,0:T(8,128)S(1)}, f32[4,128,128]{2,1,0:T(8,128)S(1)}, u32[]{:S(2)}, u32[]{:S(2)}) collective-permute-start(f32[4,128,128]{2,1,0:T(8,128)S(1)} %get-tuple-element.192), channel_id=1, source_target_pairs={{32,0},{64,32},{96,64},{0,96},{33,1},{65,33},{97,65},{1,97},{34,2}... | collective-permute-start | bytes 786440 | tf_op jit(solution)/shard_map/ppermute | solution.py:382
  (48 other events, 790.3 us)
